TPU v7x, 256 devices: a whole 4x4x8 slice. The times are simulated.
256 devices in a mesh: shot: 16 (over y, x_hi, core), slab: 16 (over z, x_lo).
Axes of the slice: x: 4 (x_hi: 2, x_lo: 2; x = x_hi * 2 + x_lo), y: 4, z: 8, core: 2. Of those that a mesh axis runs over, the one named last changes fastest.
Arguments:
- state_before: float32 [16, 256, 128, 128], P('shot', 'slab'), may hold values from -6 to 6
- state_now: float32 [16, 256, 128, 128], P('shot', 'slab'), may hold values from -6 to 6
- adjoint_after: float32 [16, 256, 128, 128], P('shot', 'slab'), may hold values from -6 to 6
- adjoint_now: float32 [16, 256, 128, 128], P('shot', 'slab'), may hold values from -6 to 6
- speed_term: float32 [256, 128, 128], P('slab'), may hold values from 0.04 to 0.18
- wavelet: float32 [16, 8], P('shot'), may hold values from -180 to 180
- source: int32 [16, 3], P('shot'), may hold values from 0 to 255, as said below
- receivers: int32 [16, 3, 4096], P('shot'), may hold values from 0 to 255, as said below
- traces: float32 [16, 8, 4096], P('shot', None, 'slab'), may hold values from -6 to 6
Outputs:
- adj_first: float32 [16, 256, 128, 128], P('shot', 'slab')
- adj_second: float32 [16, 256, 128, 128], P('shot', 'slab')
- gradient: float32 [256, 128, 128], P('slab', 'shot')
Inputs may be any that keep to these rules, and one draw needn't show every extreme that they name: `source`: row 0 is a depth row below 256, row 1 a cell below 128, row 2 a cell below 128. `receivers`: row 0 is a depth row below 256, row 1 a cell below 128, row 2 a cell below 128; several receivers may share a cell.
All inputs are finite; a program needn't handle non-finite values.
Results may differ from a plain program's by a relative error of at most 0.0003.
Values sent between devices are 32-bit elements; how exact they have to be, the bound alone decides.
A program may use at most 128 MiB of HBM per device.

v0:
```python
import jax
import jax.numpy as jnp
from jax import lax
from jax.sharding import PartitionSpec as P

stencil_weights = (-205.0 / 72.0, 8.0 / 5.0, -1.0 / 5.0, 8.0 / 315.0, -1.0 / 560.0)


def extended_2(block, sides, width):
    for axis, dim in sides:
        count = lax.axis_size(axis)
        forward = [(i, i + 1) for i in range(count - 1)]
        backward = [(target, source) for source, target in forward]
        low = lax.ppermute(
            lax.slice_in_dim(block, block.shape[dim] - width, None, axis=dim), axis, forward
        )
        high = lax.ppermute(lax.slice_in_dim(block, 0, width, axis=dim), axis, backward)
        block = jnp.concatenate([low, block, high], axis=dim)
    return block


def laplace(extended):
    count = extended.shape[0] - 8
    width_y = extended.shape[1]
    width_z = extended.shape[2]
    centre = extended[4 : 4 + count]
    sided = jnp.pad(centre, ((0, 0), (4, 4), (4, 4)))
    total = 3.0 * stencil_weights[0] * centre
    for step in range(1, 5):
        near = extended[4 + step : 4 + step + count] + extended[4 - step : 4 - step + count]
        near = (
            near
            + sided[:, 4 + step : 4 + step + width_y, 4 : 4 + width_z]
            + sided[:, 4 - step : 4 - step + width_y, 4 : 4 + width_z]
        )
        near = (
            near
            + sided[:, 4 : 4 + width_y, 4 + step : 4 + step + width_z]
            + sided[:, 4 : 4 + width_y, 4 - step : 4 - step + width_z]
        )
        total = total + stencil_weights[step] * near
    return total


def cell_index(coords, anchor, count, width_y, width_z):
    depth = coords[0] - anchor
    valid = (depth >= 0) & (depth < count)
    flat = depth * (width_y * width_z) + coords[1] * width_z + coords[2]
    return jnp.where(valid, flat, count * width_y * width_z)


def spot_field(coords, anchor, count, width_y, width_z):
    shape = (count, width_y, width_z)
    rows = lax.broadcasted_iota(jnp.int32, shape, 0) + anchor
    cols = lax.broadcasted_iota(jnp.int32, shape, 1)
    lanes = lax.broadcasted_iota(jnp.int32, shape, 2)
    hit = (rows == coords[0]) & (cols == coords[1]) & (lanes == coords[2])
    return jnp.where(hit, 1.0, 0.0).astype(jnp.float32)


def injections(listen, values, anchor, count, width_y, width_z):
    steps = values.shape[0]
    cells = count * width_y * width_z
    flat = cell_index(listen, anchor, count, width_y, width_z)
    offsets = lax.broadcasted_iota(jnp.int32, values.shape, 0) * cells
    where_to = jnp.where(flat[None, :] < cells, offsets + flat[None, :], steps * cells)
    buffer = jnp.zeros((steps * cells,), jnp.float32)
    buffer = buffer.at[where_to.reshape(-1)].add(values.reshape(-1), mode="drop")
    return buffer.reshape(steps, count, width_y, width_z)


def body(
    state_before,
    state_now,
    adjoint_after,
    adjoint_now,
    speed_term,
    wavelet,
    source,
    receivers,
    traces,
):
    count, width_y, width_z = speed_term.shape
    steps = wavelet.shape[1]
    anchor = lax.axis_index("slab") * count
    scale = 1.0 / (8.0 * steps)
    all_traces = lax.all_gather(traces[0], "slab", axis=1, tiled=True)
    spot = source[0]
    listen = receivers[0]
    wave = wavelet[0]
    zero = jnp.zeros(speed_term.shape, jnp.float32)
    core_mark = spot_field(spot, anchor, count, width_y, width_z)
    inject = injections(listen, all_traces, anchor, count, width_y, width_z)

    def advance(prev, cur):
        extended = extended_2(cur, (("slab", 0),), 4)
        lapl = laplace(extended)
        return (2.0 * cur - prev + speed_term * lapl, lapl)

    def forward(carry, amount):
        prev, cur = carry
        nxt, lapl = advance(prev, cur)
        return ((cur, nxt + amount * core_mark), lapl)

    _, stored = lax.scan(forward, (state_before[0], state_now[0]), wave)

    def backward(carry, inputs):
        later, cur, total = carry
        lapl_t, added = inputs
        nxt, _ = advance(later, cur)
        return ((cur, nxt + added, total + cur * lapl_t), None)

    (second, opening, total), _ = lax.scan(
        backward, (adjoint_after[0], adjoint_now[0], zero), (stored, inject), reverse=True
    )
    gradient = lax.psum_scatter(total * scale, "shot", scatter_dimension=1, tiled=True)
    return (opening[None], second[None], gradient)


def solution(mesh):
    return jax.shard_map(
        body,
        mesh=mesh,
        in_specs=(
            P("shot", "slab", None, None),
            P("shot", "slab", None, None),
            P("shot", "slab", None, None),
            P("shot", "slab", None, None),
            P("slab", None, None),
            P("shot", None),
            P("shot", None),
            P("shot", None, None),
            P("shot", None, "slab"),
        ),
        out_specs=(
            P("shot", "slab", None, None),
            P("shot", "slab", None, None),
            P("slab", "shot", None),
        ),
        check_vma=False,
    )
```

profile of v0, /device:TPU:32, one launch (start us, length us, event | category | flops | bytes accessed | tf_op | source)
XLA Modules:
  0.0 665.3 jit_solution(1193583421039145956)
XLA Ops:
  14.1 34.4 %all-gather = f32[1,8,4096]{2,1,0:T(8,128)S(1)} all-gather(f32[1,8,256]{2,1,0:T(8,128)S(1)} %copy-done.10), channel_id=2, replica_groups=mesh['shot'=16,'slab'=16] {'slab'}, dimensions={2}, use_global_device_ids=true | all-gather | bytes 139264 | tf_op jit(solution)/shard_map/all_gather | solution.py:87
  49.8 174.8 %scatter_custom_fusion = f32[2097152]{0:T(1024)} fusion(s32[32768]{0:T(1024)S(1)} %bitcast.46, f32[32768]{0:T(1024)S(1)} %bitcast.47, f32[]{:T(128)} %constant.160.clone.1), kind=kCustom, calls=%fused_computation.106 | custom fusion | flops 32768 | bytes 8388612 | tf_op jit(solution)/shard_map/scatter-add | solution.py:68
  224.6 172.5 %while.36 = (s32[]{:T(128)}, f32[16,128,128]{2,1,0:T(8,128)}, f32[16,128,128]{2,1,0:T(8,128)S(1)}, f32[8,16,128,128]{3,2,1,0:T(8,128)}, f32[16,128,128]{2,1,0:T(...) while((s32[]{:T(128)}, f32[16,128,128]{2,1,0:T(8,128)}, ...), condition=%wide.region_1.2_spmd.clone, body=%wide.region_0.1_spmd.clone.sunk | while | flops 9961474 | bytes 32506364 | solution.py:105
  227.4 4.8 collective-permute-start.1
  246.3 4.8 collective-permute-start.1
  265.2 4.8 collective-permute-start.1
  311.7 8.3 %collective-permute-done.1 = f32[4,128,128]{2,1,0:T(8,128)S(1)} collective-permute-done((f32[4,128,128]{2,1,0:T(8,128)}, f32[4,128,128]{2,1,0:T(8,128)S(1)}, u32[]{:S(2)}, u32[]{:S(2)}) %collective-permute-start.1) | collective-permute-done | bytes 262176 | tf_op jit(solution)/shard_map/while/body/eval_jaxpr/ppermute | solution.py:17
  328.6 4.8 collective-permute-start.1
  338.9 5.5 collective-permute-done.1
  397.2 176.2 %while.37 = (s32[]{:T(128)}, f32[16,128,128]{2,1,0:T(8,128)}, f32[16,128,128]{2,1,0:T(8,128)S(1)}, f32[16,128,128]{2,1,0:T(8,128)}, f32[16,128,128]{2,1,0:T(8,12...) while((s32[]{:T(128)}, f32[16,128,128]{2,1,0:T(8,128)}, ...), condition=%wide.region_4.5_spmd.clone, body=%wide.region_3.4_spmd.clone.sunk | while | flops 9699332 | bytes 40894752 | solution.py:113
  408.5 5.2 collective-permute-done.3
  430.2 5.3 collective-permute-done.3
  452.1 5.7 collective-permute-done.3
  463.6 4.5 collective-permute-start.2
  474.0 6.2 collective-permute-done.3
  486.1 4.5 collective-permute-start.2
  496.5 6.2 collective-permute-done.3
  508.6 4.5 collective-permute-start.2
  519.0 6.2 collective-permute-done.3
  531.0 4.5 collective-permute-start.2
  541.5 6.2 collective-permute-done.3
  553.5 4.5 collective-permute-start.2
  562.9 5.3 collective-permute-done.3
  576.1 82.3 %reduce-scatter.2.cloned.1.call-done = f32[16,8,128]{2,1,0:T(8,128)} async-done(((f32[16,128,128]{2,1,0:T(8,128)}), f32[16,8,128]{2,1,0:T(8,128)}) %reduce-scatter.2.cloned.1.call-update) | async-done | bytes 65552 | tf_op jit(solution)/shard_map/reduce_scatter | solution.py:116
  (272 shorter events, 256.2 us)
Async XLA Ops:
  7.2 651.3 %reduce-scatter.2.cloned.1.call-start = ((), (), s32[]{:S(2)}) async-start(), calls=%async_computation.1 | async-start | bytes 1114112 | tf_op jit(solution)/shard_map/reduce_scatter | solution.py:116
  227.4 10.3 %collective-permute-start.1 = (f32[4,128,128]{2,1,0:T(8,128)}, f32[4,128,128]{2,1,0:T(8,128)S(1)}, u32[]{:S(2)}, u32[]{:S(2)}) collective-permute-start(f32[4,128,128]{2,1,0:T(8,128)} %get-tuple-element.442), channel_id=1, source_target_pairs={{1,0},{2,1},{3,2},{4,3},{5,4},{6,5},{7,6},{8,7},{9,8},{10,9},{11,1... | collective-permute-start | bytes 786440 | tf_op jit(solution)/shard_map/while/body/eval_jaxpr/ppermute | solution.py:17
  246.3 10.3 %collective-permute-start.1 = (f32[4,128,128]{2,1,0:T(8,128)}, f32[4,128,128]{2,1,0:T(8,128)S(1)}, u32[]{:S(2)}, u32[]{:S(2)}) collective-permute-start(f32[4,128,128]{2,1,0:T(8,128)} %get-tuple-element.442), channel_id=1, source_target_pairs={{1,0},{2,1},{3,2},{4,3},{5,4},{6,5},{7,6},{8,7},{9,8},{10,9},{11,1... | collective-permute-start | bytes 786440 | tf_op jit(solution)/shard_map/while/body/eval_jaxpr/ppermute | solution.py:17
  265.2 10.3 %collective-permute-start.1 = (f32[4,128,128]{2,1,0:T(8,128)}, f32[4,128,128]{2,1,0:T(8,128)S(1)}, u32[]{:S(2)}, u32[]{:S(2)}) collective-permute-start(f32[4,128,128]{2,1,0:T(8,128)} %get-tuple-element.442), channel_id=1, source_target_pairs={{1,0},{2,1},{3,2},{4,3},{5,4},{6,5},{7,6},{8,7},{9,8},{10,9},{11,1... | collective-permute-start | bytes 786440 | tf_op jit(solution)/shard_map/while/body/eval_jaxpr/ppermute | solution.py:17
  305.5 14.5 %collective-permute-start.1 = (f32[4,128,128]{2,1,0:T(8,128)}, f32[4,128,128]{2,1,0:T(8,128)S(1)}, u32[]{:S(2)}, u32[]{:S(2)}) collective-permute-start(f32[4,128,128]{2,1,0:T(8,128)} %get-tuple-element.442), channel_id=1, source_target_pairs={{1,0},{2,1},{3,2},{4,3},{5,4},{6,5},{7,6},{8,7},{9,8},{10,9},{11,1... | collective-permute-start | bytes 786440 | tf_op jit(solution)/shard_map/while/body/eval_jaxpr/ppermute | solution.py:17
  326.7 11.0 %collective-permute-start = (f32[4,128,128]{2,1,0:T(8,128)}, f32[4,128,128]{2,1,0:T(8,128)}, u32[]{:S(2)}, u32[]{:S(2)}) collective-permute-start(f32[4,128,128]{2,1,0:T(8,128)} %get-tuple-element.439), channel_id=1, source_target_pairs={{0,1},{1,2},{2,3},{3,4},{4,5},{5,6},{6,7},{7,8},{8,9},{9,10},{10,1... | collective-permute-start | bytes 786440 | tf_op jit(solution)/shard_map/while/body/eval_jaxpr/ppermute | solution.py:14
  328.6 15.8 %collective-permute-start.1 = (f32[4,128,128]{2,1,0:T(8,128)}, f32[4,128,128]{2,1,0:T(8,128)S(1)}, u32[]{:S(2)}, u32[]{:S(2)}) collective-permute-start(f32[4,128,128]{2,1,0:T(8,128)} %get-tuple-element.442), channel_id=1, source_target_pairs={{1,0},{2,1},{3,2},{4,3},{5,4},{6,5},{7,6},{8,7},{9,8},{10,9},{11,1... | collective-permute-start | bytes 786440 | tf_op jit(solution)/shard_map/while/body/eval_jaxpr/ppermute | solution.py:17
  351.1 11.5 %collective-permute-start = (f32[4,128,128]{2,1,0:T(8,128)}, f32[4,128,128]{2,1,0:T(8,128)}, u32[]{:S(2)}, u32[]{:S(2)}) collective-permute-start(f32[4,128,128]{2,1,0:T(8,128)} %get-tuple-element.439), channel_id=1, source_target_pairs={{0,1},{1,2},{2,3},{3,4},{4,5},{5,6},{6,7},{7,8},{8,9},{9,10},{10,1... | collective-permute-start | bytes 786440 | tf_op jit(solution)/shard_map/while/body/eval_jaxpr/ppermute | solution.py:14
  354.3 13.8 %collective-permute-start.1 = (f32[4,128,128]{2,1,0:T(8,128)}, f32[4,128,128]{2,1,0:T(8,128)S(1)}, u32[]{:S(2)}, u32[]{:S(2)}) collective-permute-start(f32[4,128,128]{2,1,0:T(8,128)} %get-tuple-element.442), channel_id=1, source_target_pairs={{1,0},{2,1},{3,2},{4,3},{5,4},{6,5},{7,6},{8,7},{9,8},{10,9},{11,1... | collective-permute-start | bytes 786440 | tf_op jit(solution)/shard_map/while/body/eval_jaxpr/ppermute | solution.py:17
  374.8 11.1 %collective-permute-start = (f32[4,128,128]{2,1,0:T(8,128)}, f32[4,128,128]{2,1,0:T(8,128)}, u32[]{:S(2)}, u32[]{:S(2)}) collective-permute-start(f32[4,128,128]{2,1,0:T(8,128)} %get-tuple-element.439), channel_id=1, source_target_pairs={{0,1},{1,2},{2,3},{3,4},{4,5},{5,6},{6,7},{7,8},{8,9},{9,10},{10,1... | collective-permute-start | bytes 786440 | tf_op jit(solution)/shard_map/while/body/eval_jaxpr/ppermute | solution.py:14
  378.2 13.1 %collective-permute-start.1 = (f32[4,128,128]{2,1,0:T(8,128)}, f32[4,128,128]{2,1,0:T(8,128)S(1)}, u32[]{:S(2)}, u32[]{:S(2)}) collective-permute-start(f32[4,128,128]{2,1,0:T(8,128)} %get-tuple-element.442), channel_id=1, source_target_pairs={{1,0},{2,1},{3,2},{4,3},{5,4},{6,5},{7,6},{8,7},{9,8},{10,9},{11,1... | collective-permute-start | bytes 786440 | tf_op jit(solution)/shard_map/while/body/eval_jaxpr/ppermute | solution.py:17
  397.9 10.3 %collective-permute-start.2 = (f32[4,128,128]{2,1,0:T(8,128)S(1)}, f32[4,128,128]{2,1,0:T(8,128)S(1)}, u32[]{:S(2)}, u32[]{:S(2)}) collective-permute-start(f32[4,128,128]{2,1,0:T(8,128)S(1)} %get-tuple-element.452), channel_id=1, source_target_pairs={{0,1},{1,2},{2,3},{3,4},{4,5},{5,6},{6,7},{7,8},{8,9},{9,10},{10,1... | collective-permute-start | bytes 786440 | tf_op jit(solution)/shard_map/while/body/eval_jaxpr/ppermute | solution.py:14
  401.5 12.3 %collective-permute-start.3 = (f32[4,128,128]{2,1,0:T(8,128)}, f32[4,128,128]{2,1,0:T(8,128)S(1)}, u32[]{:S(2)}, u32[]{:S(2)}) collective-permute-start(f32[4,128,128]{2,1,0:T(8,128)} %get-tuple-element.455), channel_id=1, source_target_pairs={{1,0},{2,1},{3,2},{4,3},{5,4},{6,5},{7,6},{8,7},{9,8},{10,9},{11,1... | collective-permute-start | bytes 786440 | tf_op jit(solution)/shard_map/while/body/eval_jaxpr/ppermute | solution.py:17
  419.6 10.3 %collective-permute-start.2 = (f32[4,128,128]{2,1,0:T(8,128)S(1)}, f32[4,128,128]{2,1,0:T(8,128)S(1)}, u32[]{:S(2)}, u32[]{:S(2)}) collective-permute-start(f32[4,128,128]{2,1,0:T(8,128)S(1)} %get-tuple-element.452), channel_id=1, source_target_pairs={{0,1},{1,2},{2,3},{3,4},{4,5},{5,6},{6,7},{7,8},{8,9},{9,10},{10,1... | collective-permute-start | bytes 786440 | tf_op jit(solution)/shard_map/while/body/eval_jaxpr/ppermute | solution.py:14
  423.2 12.3 %collective-permute-start.3 = (f32[4,128,128]{2,1,0:T(8,128)}, f32[4,128,128]{2,1,0:T(8,128)S(1)}, u32[]{:S(2)}, u32[]{:S(2)}) collective-permute-start(f32[4,128,128]{2,1,0:T(8,128)} %get-tuple-element.455), channel_id=1, source_target_pairs={{1,0},{2,1},{3,2},{4,3},{5,4},{6,5},{7,6},{8,7},{9,8},{10,9},{11,1... | collective-permute-start | bytes 786440 | tf_op jit(solution)/shard_map/while/body/eval_jaxpr/ppermute | solution.py:17
  441.4 10.4 %collective-permute-start.2 = (f32[4,128,128]{2,1,0:T(8,128)S(1)}, f32[4,128,128]{2,1,0:T(8,128)S(1)}, u32[]{:S(2)}, u32[]{:S(2)}) collective-permute-start(f32[4,128,128]{2,1,0:T(8,128)S(1)} %get-tuple-element.452), channel_id=1, source_target_pairs={{0,1},{1,2},{2,3},{3,4},{4,5},{5,6},{6,7},{7,8},{8,9},{9,10},{10,1... | collective-permute-start | bytes 786440 | tf_op jit(solution)/shard_map/while/body/eval_jaxpr/ppermute | solution.py:14
  445.7 12.1 %collective-permute-start.3 = (f32[4,128,128]{2,1,0:T(8,128)}, f32[4,128,128]{2,1,0:T(8,128)S(1)}, u32[]{:S(2)}, u32[]{:S(2)}) collective-permute-start(f32[4,128,128]{2,1,0:T(8,128)} %get-tuple-element.455), channel_id=1, source_target_pairs={{1,0},{2,1},{3,2},{4,3},{5,4},{6,5},{7,6},{8,7},{9,8},{10,9},{11,1... | collective-permute-start | bytes 786440 | tf_op jit(solution)/shard_map/while/body/eval_jaxpr/ppermute | solution.py:17
  463.6 10.2 %collective-permute-start.2 = (f32[4,128,128]{2,1,0:T(8,128)S(1)}, f32[4,128,128]{2,1,0:T(8,128)S(1)}, u32[]{:S(2)}, u32[]{:S(2)}) collective-permute-start(f32[4,128,128]{2,1,0:T(8,128)S(1)} %get-tuple-element.452), channel_id=1, source_target_pairs={{0,1},{1,2},{2,3},{3,4},{4,5},{5,6},{6,7},{7,8},{8,9},{9,10},{10,1... | collective-permute-start | bytes 786440 | tf_op jit(solution)/shard_map/while/body/eval_jaxpr/ppermute | solution.py:14
  468.1 12.1 %collective-permute-start.3 = (f32[4,128,128]{2,1,0:T(8,128)}, f32[4,128,128]{2,1,0:T(8,128)S(1)}, u32[]{:S(2)}, u32[]{:S(2)}) collective-permute-start(f32[4,128,128]{2,1,0:T(8,128)} %get-tuple-element.455), channel_id=1, source_target_pairs={{1,0},{2,1},{3,2},{4,3},{5,4},{6,5},{7,6},{8,7},{9,8},{10,9},{11,1... | collective-permute-start | bytes 786440 | tf_op jit(solution)/shard_map/while/body/eval_jaxpr/ppermute | solution.py:17
  486.1 10.2 %collective-permute-start.2 = (f32[4,128,128]{2,1,0:T(8,128)S(1)}, f32[4,128,128]{2,1,0:T(8,128)S(1)}, u32[]{:S(2)}, u32[]{:S(2)}) collective-permute-start(f32[4,128,128]{2,1,0:T(8,128)S(1)} %get-tuple-element.452), channel_id=1, source_target_pairs={{0,1},{1,2},{2,3},{3,4},{4,5},{5,6},{6,7},{7,8},{8,9},{9,10},{10,1... | collective-permute-start | bytes 786440 | tf_op jit(solution)/shard_map/while/body/eval_jaxpr/ppermute | solution.py:14
  490.6 12.1 %collective-permute-start.3 = (f32[4,128,128]{2,1,0:T(8,128)}, f32[4,128,128]{2,1,0:T(8,128)S(1)}, u32[]{:S(2)}, u32[]{:S(2)}) collective-permute-start(f32[4,128,128]{2,1,0:T(8,128)} %get-tuple-element.455), channel_id=1, source_target_pairs={{1,0},{2,1},{3,2},{4,3},{5,4},{6,5},{7,6},{8,7},{9,8},{10,9},{11,1... | collective-permute-start | bytes 786440 | tf_op jit(solution)/shard_map/while/body/eval_jaxpr/ppermute | solution.py:17
  513.1 12.1 %collective-permute-start.3 = (f32[4,128,128]{2,1,0:T(8,128)}, f32[4,128,128]{2,1,0:T(8,128)S(1)}, u32[]{:S(2)}, u32[]{:S(2)}) collective-permute-start(f32[4,128,128]{2,1,0:T(8,128)} %get-tuple-element.455), channel_id=1, source_target_pairs={{1,0},{2,1},{3,2},{4,3},{5,4},{6,5},{7,6},{8,7},{9,8},{10,9},{11,1... | collective-permute-start | bytes 786440 | tf_op jit(solution)/shard_map/while/body/eval_jaxpr/ppermute | solution.py:17
  535.6 12.1 %collective-permute-start.3 = (f32[4,128,128]{2,1,0:T(8,128)}, f32[4,128,128]{2,1,0:T(8,128)S(1)}, u32[]{:S(2)}, u32[]{:S(2)}) collective-permute-start(f32[4,128,128]{2,1,0:T(8,128)} %get-tuple-element.455), channel_id=1, source_target_pairs={{1,0},{2,1},{3,2},{4,3},{5,4},{6,5},{7,6},{8,7},{9,8},{10,9},{11,1... | collective-permute-start | bytes 786440 | tf_op jit(solution)/shard_map/while/body/eval_jaxpr/ppermute | solution.py:17
  558.0 10.2 %collective-permute-start.3 = (f32[4,128,128]{2,1,0:T(8,128)}, f32[4,128,128]{2,1,0:T(8,128)S(1)}, u32[]{:S(2)}, u32[]{:S(2)}) collective-permute-start(f32[4,128,128]{2,1,0:T(8,128)} %get-tuple-element.455), channel_id=1, source_target_pairs={{1,0},{2,1},{3,2},{4,3},{5,4},{6,5},{7,6},{8,7},{9,8},{10,9},{11,1... | collective-permute-start | bytes 786440 | tf_op jit(solution)/shard_map/while/body/eval_jaxpr/ppermute | solution.py:17
  (50 other events, 926.2 us)
Sparse Core Ops, SparseCore 0:
  576.2 82.1 reduce-scatter.1
where the time goes:
time: 667 us; the launch traced here: 665 us
  other arithmetic  247 us (37%)
  waiting for transfers between devices  205 us (31%)
  starting transfers between devices  108 us (16%)
  local copies, waits for them, and re-layouts  55 us (8%)
  blocking collectives  34.4 us (5%)
  between operations  14.2 us (2%)
    scatter-add x1, other arithmetic, injections(): buffer.at[where_to.reshape(-1)].add(values.reshape(-1), mode='drop')  175 us
    reduce_scatter x1, waiting for transfers between devices, body(): lax.psum_scatter(total * scale, 'shot', scatter_dimension=1, tiled=True)  82.3 us
    ppermute x16, waiting for transfers between devices, extended_2(): lax.ppermute(lax.slice_in_dim(block, 0, width, axis=dim), axis, backward)  73.9 us
    ppermute x16, starting transfers between devices, extended_2(): lax.ppermute(lax.slice_in_dim(block, block.shape[dim] - width, None, axis...  56 us
    ppermute x16, starting transfers between devices, extended_2(): lax.ppermute(lax.slice_in_dim(block, 0, width, axis=dim), axis, backward)  51.7 us
    ppermute x16, waiting for transfers between devices, extended_2(): lax.ppermute(lax.slice_in_dim(block, block.shape[dim] - width, None, axis...  48.9 us
    all_gather x1, blocking collectives, body(): all_traces = lax.all_gather(traces[0], 'slab', axis=1, tiled=True)  34.4 us
    while x128, local copies, waits for them, and re-layouts  30.9 us
  transfers between devices with their start and end apart: 33, of which 33 were waited for; matrix products, arithmetic and copies ran while one was open for 3% of the time, Pallas kernels for 0%

commit v1 on v0

v1 whole, which is shorter than its diff:
```python
import functools

import numpy as np
import jax
import jax.numpy as jnp
from jax import lax
from jax.experimental import pallas as pl
from jax.experimental.pallas import tpu as pltpu
from jax.sharding import PartitionSpec as P

MESH = pl.DeviceIdType.MESH
F32 = jnp.float32
BF16 = jnp.bfloat16

UNIT = 8.0 / 5.0
CENTRE = 3.0 * (-205.0 / 72.0) / UNIT
FAR = 1.0 / 63.0
EDGE = 4


def band(width):
    gap = np.abs(np.arange(width)[:, None] - np.arange(width)[None, :])
    near = np.where(gap == 1, 1.0, 0.0) + np.where(gap == 2, -1.0 / 8.0, 0.0)
    far = np.where(gap == 3, 1.0, 0.0) + np.where(gap == 4, -9.0 / 128.0, 0.0)
    row = np.concatenate([near, far], axis=1)
    return np.concatenate([row, row], axis=0)


def place():
    shot = lax.axis_index("shot")
    slab = lax.axis_index("slab")
    return shot, slab, lax.rem(shot, 2), lax.rem(slab, 2)


def gather_kernel(slabs, traces, cells, all_traces, all_cells, send, recv, own, pack_send, pack_recv, pack_own):
    shot, slab, core, side = place()
    half = slabs // 2
    z = lax.div(slab, 2)
    stays = core == side
    barrier = pltpu.get_barrier_semaphore()

    @pl.loop(0, slabs)
    def _(k):
        @pl.when(jnp.logical_or(core != side, k != slab))
        def _():
            pl.semaphore_signal(barrier, inc=1, device_id=(shot - core + side, k), device_id_type=MESH)

    pl.semaphore_wait(barrier, jnp.where(stays, slabs - 1, slabs))

    def outgoing(k):
        to_core, to_z = lax.div(k, half), lax.rem(k, half)
        return pltpu.make_async_remote_copy(
            src_ref=traces,
            dst_ref=all_traces.at[slab],
            send_sem=send.at[k],
            recv_sem=recv.at[slab],
            device_id=(shot - core + to_core, 2 * to_z + core),
            device_id_type=MESH,
        )

    def is_me(k):
        return jnp.logical_and(stays, k == core * half + z)

    mine = pltpu.make_async_copy(traces, all_traces.at[slab], own.at[0])
    pack = pltpu.make_async_remote_copy(
        src_ref=cells,
        dst_ref=all_cells,
        send_sem=pack_send.at[0],
        recv_sem=pack_recv.at[0],
        device_id=(shot + 1 - 2 * core, slab),
        device_id_type=MESH,
    )
    pack_mine = pltpu.make_async_copy(cells, all_cells, pack_own.at[0])

    @pl.when(stays)
    def _():
        pack.start()
        pack_mine.start()
        mine.start()

    @pl.loop(0, slabs)
    def _(k):
        @pl.when(jnp.logical_not(is_me(k)))
        def _():
            outgoing(k).start()

    @pl.loop(0, slabs)
    def _(k):
        @pl.when(jnp.logical_or(core != side, k != slab))
        def _():
            pltpu.make_async_remote_copy(
                src_ref=traces,
                dst_ref=all_traces.at[k],
                send_sem=send.at[k],
                recv_sem=recv.at[k],
                device_id=(shot - core + side, k),
                device_id_type=MESH,
            ).wait_recv()

    @pl.loop(0, slabs)
    def _(k):
        @pl.when(jnp.logical_not(is_me(k)))
        def _():
            outgoing(k).wait_send()

    @pl.when(stays)
    def _():
        pack.wait_send()
        pack_mine.wait()
        mine.wait()

    @pl.when(jnp.logical_not(stays))
    def _():
        pack.wait_recv()


def inject_kernel(cells, keys, traces, out, listed):
    @pl.loop(0, cells // 16)
    def _(i):
        out[pl.ds(pl.multiple_of(i * 128, 128), 128), :] = jnp.zeros((128, 128), F32)

    rows, lanes = keys.shape

    def compact(i, count):
        for u in range(16):
            key = keys[lax.shift_right_logical(i, 3), jnp.bitwise_and(i, 7) * 16 + u]
            listed[count] = key
            count = count + jnp.where(key >= 0, 1, 0).astype(jnp.int32)
        return count

    count = lax.fori_loop(0, rows * lanes // 16, compact, jnp.int32(0))
    lane = lax.broadcasted_iota(jnp.int32, (8, 128), 1)

    def add(k, carry):
        key = listed[k]
        r = lax.shift_right_logical(key, 18)
        cell = jnp.bitwise_and(key, (1 << 18) - 1)
        z = jnp.bitwise_and(cell, 127)
        row = pl.multiple_of(lax.shift_right_logical(cell, 7) * 8, 8)
        column = pl.multiple_of(jnp.bitwise_and(lax.shift_right_logical(r, 7), 1) * 128, 128)
        values = traces[lax.shift_right_logical(r, 8), :, pl.ds(column, 128)]
        turned = pltpu.roll(values, jnp.bitwise_and(z - jnp.bitwise_and(r, 127), 127), 1)
        out[pl.ds(row, 8), :] = out[pl.ds(row, 8), :] + jnp.where(lane == z, turned, 0.0)
        return carry

    lax.fori_loop(0, count, add, jnp.int32(0))


def wave_kernel(
    shots,
    slabs,
    steps,
    scale,
    adj_now,
    adj_now_far,
    adj_after,
    adj_after_far,
    state_now,
    state_before,
    speed,
    speed_far,
    added,
    amounts,
    mark,
    weights_z,
    weights_y,
    opening,
    second,
    gradient,
    qa,
    pf,
    laps,
    inj,
    spd,
    total,
    parts,
    loads,
    swap_send,
    swap_recv,
    halo_send,
    halo_recv,
    out_send,
    out_recv,
    part_send,
    part_recv,
    part_own,
):
    shot, slab, core, side = place()
    z = lax.div(slab, 2)
    stays = core == side
    moves = core != side
    count, wide, lanes = spd.shape
    mid = count - 2 * EDGE
    last = slabs // 2 - 1
    has_outer = jnp.logical_or(jnp.logical_and(core == 0, z > 0), jnp.logical_and(core == 1, z < last))
    inner = (shot + 1 - 2 * core, slab)
    outer = (shot + 1 - 2 * core, slab + 4 * core - 2)
    partner = (shot - core + side, slab - side + core)
    chunk = wide // shots
    me = shot - core + side
    own_rows = pl.ds(EDGE, count)

    def source_of(s):
        return (s - lax.rem(s, 2) + side, 2 * z + lax.rem(s, 2))

    barrier = pltpu.get_barrier_semaphore()
    pl.semaphore_signal(barrier, inc=1, device_id=inner, device_id_type=MESH)

    @pl.when(has_outer)
    def _():
        pl.semaphore_signal(barrier, inc=1, device_id=outer, device_id_type=MESH)

    @pl.when(moves)
    def _():
        pl.semaphore_signal(barrier, inc=1, device_id=partner, device_id_type=MESH)

    @pl.loop(0, shots)
    def _(s):
        @pl.when(jnp.logical_or(moves, s != shot))
        def _():
            pl.semaphore_signal(barrier, inc=1, device_id=source_of(s), device_id_type=MESH)

    def load(k, near, far, to):
        def go():
            @pl.when(stays)
            def _():
                pltpu.make_async_copy(near, to, loads.at[k]).start()

            @pl.when(moves)
            def _():
                pltpu.make_async_copy(far, to, loads.at[k]).start()

        def done():
            pltpu.make_async_copy(near, to, loads.at[k]).wait()

        return go, done

    now_go, now_done = load(0, adj_now, adj_now_far, qa.at[1, own_rows])
    after_go, after_done = load(1, adj_after, adj_after_far, qa.at[0, own_rows])
    speed_go, speed_done = load(2, speed, speed_far, spd)
    now_go()
    speed_go()
    after_go()
    inj_copy = pltpu.make_async_copy(added, inj, loads.at[3])
    inj_copy.start()

    def swap(k, here, to):
        remote = pltpu.make_async_remote_copy(
            src_ref=here,
            dst_ref=to,
            send_sem=swap_send.at[k],
            recv_sem=swap_recv.at[k],
            device_id=partner,
            device_id_type=MESH,
        )
        local = pltpu.make_async_copy(here, to, loads.at[4 + k])

        def go():
            @pl.when(moves)
            def _():
                remote.start()

            @pl.when(stays)
            def _():
                local.start()

        def done():
            @pl.when(moves)
            def _():
                remote.wait_recv()

            @pl.when(stays)
            def _():
                local.wait()

        def sent():
            @pl.when(moves)
            def _():
                remote.wait_send()

        return go, done, sent

    p_now = swap(0, state_now, pf.at[1, own_rows])
    p_before = swap(1, state_before, pf.at[0, own_rows])

    @pl.when(jnp.logical_not(has_outer))
    def _():
        @pl.loop(0, steps)
        def _(k):
            @pl.loop(0, EDGE)
            def _(r):
                row = core * (count + EDGE) + r
                qa[k + 1, row] = jnp.zeros((wide, lanes), F32)
                pf[k + 1, row] = jnp.zeros((wide, lanes), F32)

    pl.semaphore_wait(
        barrier,
        1 + jnp.where(has_outer, 1, 0) + jnp.where(moves, 1, 0) + jnp.where(stays, shots - 1, shots),
    )

    fields = (qa, pf)

    def inner_copy(chain, slot):
        return pltpu.make_async_remote_copy(
            src_ref=fields[chain].at[slot, pl.ds(count - core * mid - core * EDGE, EDGE)],
            dst_ref=fields[chain].at[slot, pl.ds(core * (count + EDGE), EDGE)],
            send_sem=halo_send.at[chain, 0, slot],
            recv_sem=halo_recv.at[chain, 0, slot],
            device_id=inner,
            device_id_type=MESH,
        )

    def outer_copy(chain, slot):
        return pltpu.make_async_remote_copy(
            src_ref=fields[chain].at[slot, pl.ds(EDGE + core * (mid + EDGE), EDGE)],
            dst_ref=fields[chain].at[slot, pl.ds((1 - core) * (count + EDGE), EDGE)],
            send_sem=halo_send.at[chain, 1, slot],
            recv_sem=halo_recv.at[chain, 1, slot],
            device_id=outer,
            device_id_type=MESH,
        )

    def send_inner(chain, slot):
        inner_copy(chain, slot).start()

    def send_outer(chain, slot):
        @pl.when(has_outer)
        def _():
            outer_copy(chain, slot).start()

    def wait_inner(chain, slot):
        inner_copy(chain, slot).wait_recv()

    def wait_outer(chain, slot):
        @pl.when(has_outer)
        def _():
            outer_copy(chain, slot).wait_recv()

    inner_base = (1 - core) * (mid + EDGE)
    outer_base = core * (mid + EDGE)

    def lateral(field, slot, group, finish):
        x = field[slot, pl.ds(EDGE + 4 * group, 4)]
        high = x.astype(BF16)
        low = (x - high.astype(F32)).astype(BF16)
        along = jnp.concatenate([high.reshape(4 * wide, lanes), low.reshape(4 * wide, lanes)], axis=1)
        across = jnp.concatenate(
            [
                jnp.concatenate([high[i] for i in range(4)], axis=1),
                jnp.concatenate([low[i] for i in range(4)], axis=1),
            ],
            axis=0,
        )
        sums_z = jnp.dot(along, weights_z[...], preferred_element_type=F32)
        sums_y = jnp.dot(weights_y[...], across, preferred_element_type=F32)
        for i in range(4):
            near = sums_z[wide * i : wide * (i + 1), :lanes] + sums_y[:wide, lanes * i : lanes * (i + 1)]
            far = sums_z[wide * i : wide * (i + 1), lanes:] + sums_y[wide:, lanes * i : lanes * (i + 1)]
            finish(4 * group + i, x[i], near + far * FAR + CENTRE * x[i])

    def depth(field, slot, base, planes, finish):
        @pl.loop(0, wide // 8)
        def _(k):
            part = pl.ds(pl.multiple_of(8 * k, 8), 8)
            e = [field[slot, base + r, part, :] for r in range(planes + 2 * EDGE)]
            for r in range(planes):
                value = (e[r + 3] + e[r + 5]) - 0.125 * (e[r + 2] + e[r + 6])
                value = value + FAR * ((e[r + 1] + e[r + 7]) - (9.0 / 128.0) * (e[r] + e[r + 8]))
                finish(base + r, part, value)

    def lateral_a(j):
        def finish(row, x, value):
            extra = inj[pl.ds(row * (8 * wide) + (steps - 1 - j), wide, stride=8), :]
            qa[j + 2, EDGE + row] = (2.0 * x - qa[j, EDGE + row]) + extra + spd[row] * value

        @pl.loop(0, count // 4)
        def _(group):
            lateral(qa, j + 1, group, finish)

        depth_a(j, EDGE, mid)

    def depth_a(j, base, planes):
        def finish(row, part, value):
            qa[j + 2, EDGE + row, part, :] = qa[j + 2, EDGE + row, part, :] + spd[row, part, :] * value

        depth(qa, j + 1, base, planes, finish)

    def edges_a(j, more):
        wait_inner(0, j + 1)
        depth_a(j, inner_base, EDGE)
        if more is None:
            send_inner(0, j + 2)
        else:
            pl.when(more)(lambda: send_inner(0, j + 2))
        wait_outer(0, j + 1)
        depth_a(j, outer_base, EDGE)
        if more is None:
            send_outer(0, j + 2)
        else:
            pl.when(more)(lambda: send_outer(0, j + 2))

    lead = steps // 2

    def lateral_f(i, kept):
        keep = i if kept else lead

        def finish(row, x, value):
            pf[i + 2, EDGE + row] = (2.0 * x - pf[i, EDGE + row]) + amounts[i, row] * mark[...]
            laps[keep, row] = value

        @pl.loop(0, count // 4)
        def _(group):
            lateral(pf, i + 1, group, finish)

        depth_f(i, EDGE, mid, kept)

    def depth_f(i, base, planes, kept):
        keep = i if kept else lead

        def finish(row, part, value):
            lap = laps[keep, row, part, :] + value
            pf[i + 2, EDGE + row, part, :] = pf[i + 2, EDGE + row, part, :] + spd[row, part, :] * lap
            if kept:
                laps[keep, row, part, :] = lap
            else:
                total[row, part, :] = total[row, part, :] + qa[steps - i, EDGE + row, part, :] * lap

        depth(pf, i + 1, base, planes, finish)

    def edges_f(i, kept, more):
        wait_inner(1, i + 1)
        depth_f(i, inner_base, EDGE, kept)
        if more:
            send_inner(1, i + 2)
        wait_outer(1, i + 1)
        depth_f(i, outer_base, EDGE, kept)
        if more:
            send_outer(1, i + 2)

    p_now[0]()
    now_done()
    send_outer(0, 1)
    send_inner(0, 1)
    p_before[0]()
    after_done()
    speed_done()

    @pl.loop(0, count)
    def _(row):
        spd[row] = UNIT * spd[row]

    inj_copy.wait()
    lateral_a(0)

    @pl.loop(0, lead)
    def _(j):
        edges_a(j, None)
        lateral_a(j + 1)

    p_now[1]()
    send_outer(1, 1)
    send_inner(1, 1)
    p_before[1]()
    lateral_f(0, True)

    def result(k, here, to):
        remote = pltpu.make_async_remote_copy(
            src_ref=here,
            dst_ref=to,
            send_sem=out_send.at[k],
            recv_sem=out_recv.at[k],
            device_id=partner,
            device_id_type=MESH,
        )
        local = pltpu.make_async_copy(here, to, loads.at[6 + k])

        def go():
            @pl.when(moves)
            def _():
                remote.start()

            @pl.when(stays)
            def _():
                local.start()

        def done():
            @pl.when(moves)
            def _():
                remote.wait()

            @pl.when(stays)
            def _():
                local.wait()

        return go, done

    second_out = result(0, qa.at[steps, own_rows], second.at[0])
    opening_out = result(1, qa.at[steps + 1, own_rows], opening.at[0])

    @pl.loop(0, steps - lead)
    def _(m):
        j = lead + m
        edges_a(j, j < steps - 1)

        @pl.when(j == steps - 2)
        def _():
            second_out[0]()

        edges_f(m, True, True)

        @pl.when(j < steps - 1)
        def _():
            lateral_a(j + 1)

        @pl.when(m < lead - 1)
        def _():
            lateral_f(m + 1, True)

    opening_out[0]()

    @pl.loop(0, count)
    def _(row):
        sums = qa[steps, EDGE + row] * laps[0, row]
        for i in range(1, lead):
            sums = sums + qa[steps - i, EDGE + row] * laps[i, row]
        total[row] = sums

    lateral_f(lead, False)

    @pl.loop(lead, steps - 1)
    def _(i):
        edges_f(i, False, True)
        lateral_f(i + 1, False)

    spans = ((EDGE, mid), (0, EDGE), (EDGE + mid, EDGE))

    def is_me(s):
        return jnp.logical_and(stays, s == shot)

    def part_copy(n, s):
        rows = pl.ds(*spans[n])
        return pltpu.make_async_remote_copy(
            src_ref=total.at[rows, pl.ds(pl.multiple_of(chunk * s, chunk), chunk)],
            dst_ref=parts.at[me, rows],
            send_sem=part_send.at[n, s],
            recv_sem=part_recv.at[n, me],
            device_id=(s, 2 * z + core),
            device_id_type=MESH,
        )

    def part_mine(n):
        rows = pl.ds(*spans[n])
        return pltpu.make_async_copy(
            total.at[rows, pl.ds(pl.multiple_of(chunk * shot, chunk), chunk)], parts.at[me, rows], part_own.at[n]
        )

    def send_parts(n):
        @pl.when(stays)
        def _():
            part_mine(n).start()

        @pl.loop(0, shots)
        def _(k):
            s = lax.rem(shot + k, shots)

            @pl.when(jnp.logical_not(is_me(s)))
            def _():
                part_copy(n, s).start()

    def wait_parts(n):
        rows = pl.ds(*spans[n])

        @pl.when(stays)
        def _():
            part_mine(n).wait()

        @pl.loop(0, shots)
        def _(s):
            @pl.when(jnp.logical_or(moves, s != me))
            def _():
                pltpu.make_async_remote_copy(
                    src_ref=total.at[rows, pl.ds(0, chunk)],
                    dst_ref=parts.at[s, rows],
                    send_sem=part_send.at[n, s],
                    recv_sem=part_recv.at[n, s],
                    device_id=source_of(s),
                    device_id_type=MESH,
                ).wait_recv()

            @pl.when(jnp.logical_not(is_me(s)))
            def _():
                part_copy(n, s).wait_send()

    send_parts(0)
    edges_f(steps - 1, False, False)
    send_parts(1)
    send_parts(2)

    p_now[2]()
    p_before[2]()

    @pl.loop(1, steps + 1)
    def _(slot):
        for chain in range(2):
            inner_copy(chain, slot).wait_send()

            @pl.when(has_outer)
            def _():
                outer_copy(chain, slot).wait_send()

    second_out[1]()
    opening_out[1]()
    for n in range(3):
        wait_parts(n)

    @pl.loop(0, count)
    def _(row):
        sums = parts[0, row]
        for s in range(1, shots):
            sums = sums + parts[s, row]
        gradient[row] = sums * scale


def body(
    shots,
    slabs,
    state_before,
    state_now,
    adjoint_after,
    adjoint_now,
    speed_term,
    wavelet,
    source,
    receivers,
    traces,
):
    count, wide, lanes = speed_term.shape
    steps = wavelet.shape[1]
    held = traces.shape[2]
    plane = wide * lanes
    shot, slab, core, side = place()
    slab_here = slab - side + core

    over = ("shot", "slab")
    pairs, speed_pairs = [], []
    for s in range(shots):
        for k in range(slabs):
            c, d = s % 2, k % 2
            if c != d:
                pairs.append((s * slabs + k, (s - c + d) * slabs + k - d + c))
                high = (s // 2) % 2
                other = s - 2 * high + 2 * (1 - high) - c + d
                speed_pairs.append((s * slabs + k, other * slabs + k - d + c))
    now_far = lax.ppermute(adjoint_now[0], over, pairs)
    speed_far = lax.ppermute(speed_term, over, speed_pairs)
    after_far = lax.ppermute(adjoint_after[0], over, pairs)

    flat = (receivers[0, 0] * plane + receivers[0, 1] * lanes + receivers[0, 2]).reshape(-1, 128)
    spot = source[0, 0] * plane + source[0, 1] * lanes + source[0, 2]
    cells = jnp.concatenate([flat, jnp.broadcast_to(spot, (8, 128))], axis=0)
    wave = jnp.broadcast_to(wavelet[0][:, None], (steps, 128))
    packed = jnp.concatenate([traces[0], wave], axis=1)
    anywhere = pl.BlockSpec(memory_space=pl.ANY)
    in_vmem = pl.BlockSpec(memory_space=pltpu.VMEM)
    in_smem = pl.BlockSpec(memory_space=pltpu.SMEM)

    all_traces, all_cells = pl.pallas_call(
        functools.partial(gather_kernel, slabs),
        name="gather_traces",
        out_shape=(
            jax.ShapeDtypeStruct((slabs, steps, held + 128), F32),
            jax.ShapeDtypeStruct(cells.shape, jnp.int32),
        ),
        in_specs=[anywhere, anywhere],
        out_specs=(anywhere, anywhere),
        scratch_shapes=[
            pltpu.SemaphoreType.DMA((slabs,)),
            pltpu.SemaphoreType.DMA((slabs,)),
            pltpu.SemaphoreType.DMA((1,)),
            pltpu.SemaphoreType.DMA((1,)),
            pltpu.SemaphoreType.DMA((1,)),
            pltpu.SemaphoreType.DMA((1,)),
        ],
        compiler_params=pltpu.CompilerParams(collective_id=0, has_side_effects=True),
        cost_estimate=pl.CostEstimate(flops=0, bytes_accessed=20 << 20, transcendentals=0),
    )(packed, cells)

    base = slab_here * (count * plane)
    here = all_cells[:-8] - base
    order = lax.broadcasted_iota(jnp.int32, here.shape, 0) * 128 + lax.broadcasted_iota(jnp.int32, here.shape, 1)
    keys = jnp.where((here >= 0) & (here < count * plane), order * (count * plane) + here, -1)
    added = pl.pallas_call(
        functools.partial(inject_kernel, count * wide),
        name="inject",
        out_shape=jax.ShapeDtypeStruct((count * wide * steps, lanes), F32),
        in_specs=[in_smem, in_vmem],
        out_specs=in_vmem,
        scratch_shapes=[pltpu.SMEM((here.size,), jnp.int32)],
        compiler_params=pltpu.CompilerParams(vmem_limit_bytes=32 << 20),
        cost_estimate=pl.CostEstimate(flops=0, bytes_accessed=30 << 20, transcendentals=0),
    )(keys, all_traces)

    spot_here = all_cells[-1, 0] - base
    spot_row = jnp.where(spot_here < 0, -1, spot_here // plane)
    spot_cell = jnp.bitwise_and(spot_here, plane - 1)
    amounts = jnp.where(lax.broadcasted_iota(jnp.int32, (steps, count), 1) == spot_row, all_traces[0, :, held : held + 1], 0.0)
    mark_at = lax.broadcasted_iota(jnp.int32, (wide, lanes), 0) * lanes + lax.broadcasted_iota(jnp.int32, (wide, lanes), 1)
    mark = jnp.where(mark_at == spot_cell, 1.0, 0.0).astype(F32)
    weights = band(wide)

    long = count + 2 * EDGE
    opening, second, gradient = pl.pallas_call(
        functools.partial(wave_kernel, shots, slabs, steps, UNIT / (8.0 * steps)),
        name="waves",
        out_shape=(
            jax.ShapeDtypeStruct((1, count, wide, lanes), F32),
            jax.ShapeDtypeStruct((1, count, wide, lanes), F32),
            jax.ShapeDtypeStruct((count, wide // shots, lanes), F32),
        ),
        in_specs=[anywhere] * 9 + [in_smem, in_vmem, in_vmem, in_vmem],
        out_specs=(anywhere, anywhere, in_vmem),
        scratch_shapes=[
            pltpu.VMEM((steps + 2, long, wide, lanes), F32),
            pltpu.VMEM((steps + 2, long, wide, lanes), F32),
            pltpu.VMEM((steps // 2 + 1, count, wide, lanes), F32),
            pltpu.VMEM((count * wide * steps, lanes), F32),
            pltpu.VMEM((count, wide, lanes), F32),
            pltpu.VMEM((count, wide, lanes), F32),
            pltpu.VMEM((shots, count, wide // shots, lanes), F32),
            pltpu.SemaphoreType.DMA((8,)),
            pltpu.SemaphoreType.DMA((2,)),
            pltpu.SemaphoreType.DMA((2,)),
            pltpu.SemaphoreType.DMA((2, 2, steps + 2)),
            pltpu.SemaphoreType.DMA((2, 2, steps + 2)),
            pltpu.SemaphoreType.DMA((2,)),
            pltpu.SemaphoreType.DMA((2,)),
            pltpu.SemaphoreType.DMA((3, shots)),
            pltpu.SemaphoreType.DMA((3, shots)),
            pltpu.SemaphoreType.DMA((3,)),
        ],
        compiler_params=pltpu.CompilerParams(
            collective_id=1, has_side_effects=True, vmem_limit_bytes=62 << 20
        ),
    )(
        adjoint_now[0],
        now_far,
        adjoint_after[0],
        after_far,
        state_now[0],
        state_before[0],
        speed_term,
        speed_far,
        added,
        amounts,
        mark,
        jnp.asarray(weights, BF16),
        jnp.asarray(weights.T, BF16),
    )
    return opening, second, gradient


def solution(mesh):
    return jax.shard_map(
        functools.partial(body, mesh.shape["shot"], mesh.shape["slab"]),
        mesh=mesh,
        in_specs=(
            P("shot", "slab", None, None),
            P("shot", "slab", None, None),
            P("shot", "slab", None, None),
            P("shot", "slab", None, None),
            P("slab", None, None),
            P("shot", None),
            P("shot", None),
            P("shot", None, None),
            P("shot", None, "slab"),
        ),
        out_specs=(
            P("shot", "slab", None, None),
            P("shot", "slab", None, None),
            P("slab", "shot", None),
        ),
        check_vma=False,
    )
```

time: 667 us -> 189 us (0.28)
  other arithmetic: 247 us -> 4.27 us
  waiting for transfers between devices: 205 us -> 0.01 us
  Pallas kernels: 0 us -> 161 us
  starting transfers between devices: 108 us -> 4.07 us
  local copies, waits for them, and re-layouts: 55 us -> 15.2 us
  blocking collectives: 34.4 us -> 0 us
  between operations: 14.2 us -> 3.34 us
    scatter-add x1 -> x0, other arithmetic: 175 us -> none  [injections(): buffer.at[where_to.reshape(-1)].add(values.reshape(-1), mode='drop')]
    pallas_call x0 -> x3, Pallas kernels: none -> 161 us  [the longest x1 93.1 us: body(): pl.pallas_call(functools.partial(wave_kernel, shots, slabs, steps, UNIT /...]
    ppermute x32 -> x3, waiting for transfers between devices: 123 us -> 0.01 us  [the longest x1 0.01 us: body(): after_far = lax.ppermute(adjoint_after[0], over, pairs)]
    ppermute x32 -> x3, starting transfers between devices: 108 us -> 4.07 us  [the longest x1 1.72 us: body(): now_far = lax.ppermute(adjoint_now[0], over, pairs)]
    reduce_scatter x1 -> x0, waiting for transfers between devices: 82.3 us -> none  [body(): lax.psum_scatter(total * scale, 'shot', scatter_dimension=1, tiled=True)]
    add x16 -> x1, other arithmetic: 41.6 us -> 0.79 us  [body(): receivers[0, 0] * plane + receivers[0, 1] * lanes + receivers[0, 2]]
    all_gather x1 -> x0, blocking collectives: 34.4 us -> none  [body(): all_traces = lax.all_gather(traces[0], 'slab', axis=1, tiled=True)]
    while x128 -> x0, local copies, waits for them, and re-layouts: 30.9 us -> none
  transfers between devices with their start and end apart: 33 -> 3, of which waited for: 33 -> 0; matrix products, arithmetic and copies ran while one was open for 3% -> 4% of each run, Pallas kernels for 0% -> 36%
where the time goes in v1:
time: 189 us; the launch traced here: 188 us
  Pallas kernels  161 us (85%)
  local copies, waits for them, and re-layouts  15.2 us (8%)
  other arithmetic  4.27 us (2%)
  starting transfers between devices  4.07 us (2%)
  between operations  3.34 us (2%)
    pallas_call x1, Pallas kernels, body(): pl.pallas_call(functools.partial(wave_kernel, shots, slabs, steps, UNIT /...  93.1 us
    pallas_call x1, Pallas kernels, body(): pl.pallas_call(functools.partial(inject_kernel, count * wide), name='inje...  48.3 us
    pallas_call x1, Pallas kernels, body(): pl.pallas_call(functools.partial(gather_kernel, slabs), name='gather_trac...  19.2 us
    unnamed x9, local copies, waits for them, and re-layouts  11.2 us
  transfers between devices with their start and end apart: 3, of which 0 were waited for; matrix products, arithmetic and copies ran while one was open for 4% of the time, Pallas kernels for 36%

profile of v1, /device:TPU:32, one launch (start us, length us, event | category | flops | bytes accessed | tf_op | source)
XLA Modules:
  0.0 187.6 jit_solution(11544054749819275164)
XLA Ops:
  0.6 0.7 collective-permute-start.1
  1.4 1.7 collective-permute-start
  3.1 1.6 collective-permute-start.2
  4.7 1.4 fusion.1
  6.1 0.8 slice_add_fusion
  6.9 0.7 broadcast_in_dim.35
  7.7 1.3 pad_maximum_fusion.traces
  10.9 0.6 concatenate.7.cells
  11.6 19.2 %gather_traces.1 = (f32[16,8,384]{2,1,0:T(8,128)}, s32[40,128]{1,0:T(8,128)}) custom-call(f32[8,384]{1,0:T(8,128)} %pad_maximum_fusion.traces, s32[40,128]{1,0:T(8,128)} %concatenate.7.cells), custom_call_target="tpu_custom_call" | custom-call | bytes 20971520 | tf_op jit(solution)/shard_map/gather_traces/pallas_call | solution.py:667
  30.8 1.2 slice.34
  32.7 0.8 add_select_fusion.keys
  33.5 0.9 copy-done.1
  34.4 48.3 %inject.1.added = f32[16384,128]{1,0:T(8,128)S(1)} custom-call(s32[32,128]{1,0:T(8,128)S(1)} %add_select_fusion.keys, f32[16,8,384]{2,1,0:T(8,128)S(1)} %copy-done.1), custom_call_target="tpu_custom_call" | custom-call | bytes 31457280 | tf_op jit(solution)/shard_map/inject/pallas_call | solution.py:692
  82.7 3.2 %copy-done = f32[16384,128]{1,0:T(8,128)} copy-done((f32[16384,128]{1,0:T(8,128)}, f32[16384,128]{1,0:T(8,128)S(1)}, u32[]{:S(2)}) %copy-start) | copy-done | bytes 8388632
  85.9 0.1 slice_reduce_fusion
  86.1 0.7 broadcast_select_fusion.amounts
  86.7 0.7 fusion.mark
  87.4 0.0 collective-permute-done.1.adj_after_far
  87.4 0.0 collective-permute-done.adj_now_far
  87.5 1.0 copy-done.2
  88.4 93.1 %waves.1 = (f32[1,16,128,128]{3,2,1,0:T(8,128)}, f32[1,16,128,128]{3,2,1,0:T(8,128)}, f32[16,8,128]{2,1,0:T(8,128)}) custom-call(f32[16,128,128]{2,1,0:T(8,128)} %bitcast.10, f32[16,128,128]{2,1,0:T(8,128)} %collective-permute-done.adj_now_far, f32[16,128,128]{2,1,0:T(8,128)} %bitcast.12, f32[16,128,128]{2,1,0:T(8,128)} %copy-done.2, ...), custom_call_target="tpu_custom_call" | custom-call | tf_op jit(solution)/shard_map/waves/pallas_call | solution.py:712
  181.5 2.3 %copy.17 = f32[1,16,128,128]{3,2,1,0:T(8,128)} copy(f32[1,16,128,128]{3,2,1,0:T(8,128)} %get-tuple-element.13) | data formatting | bytes 2097152
  183.8 2.3 %copy.18 = f32[1,16,128,128]{3,2,1,0:T(8,128)} copy(f32[1,16,128,128]{3,2,1,0:T(8,128)} %get-tuple-element.14) | data formatting | bytes 2097152
  186.1 1.5 copy.19
  (7 shorter events, 0.0 us)
Async XLA Ops:
  0.6 86.8 %collective-permute-start.1 = (f32[16,128,128]{2,1,0:T(8,128)}, f32[16,128,128]{2,1,0:T(8,128)S(1)}, u32[]{:S(2)}, u32[]{:S(2)}) collective-permute-start(f32[16,128,128]{2,1,0:T(8,128)} %bitcast.11), channel_id=1, source_target_pairs={{1,16},{3,18},{5,20},{7,22},{9,24},{11,26},{13,28},{15,30},{16,1},... | collective-permute-start | bytes 3145736 | tf_op jit(solution)/shard_map/ppermute | solution.py:656
  1.4 86.1 %collective-permute-start = (f32[16,128,128]{2,1,0:T(8,128)}, f32[16,128,128]{2,1,0:T(8,128)}, u32[]{:S(2)}, u32[]{:S(2)}) collective-permute-start(f32[16,128,128]{2,1,0:T(8,128)} %bitcast.9), channel_id=1, source_target_pairs={{1,16},{3,18},{5,20},{7,22},{9,24},{11,26},{13,28},{15,30},{16,1},... | collective-permute-start | bytes 3145736 | tf_op jit(solution)/shard_map/ppermute | solution.py:654
  3.1 84.4 %collective-permute-start.2 = (f32[16,128,128]{2,1,0:T(8,128)}, f32[16,128,128]{2,1,0:T(8,128)}, u32[]{:S(2)}, u32[]{:S(2)}) collective-permute-start(f32[16,128,128]{2,1,0:T(8,128)} %speed.1), channel_id=1, source_target_pairs={{1,48},{3,50},{5,52},{7,54},{9,56},{11,58},{13,60},{15,62},{16,33}... | collective-permute-start | bytes 3145736 | tf_op jit(solution)/shard_map/ppermute | solution.py:655
  33.5 0.9 copy-start.1
  82.7 3.2 %copy-start = (f32[16384,128]{1,0:T(8,128)}, f32[16384,128]{1,0:T(8,128)S(1)}, u32[]{:S(2)}) copy-start(f32[16384,128]{1,0:T(8,128)S(1)} %inject.1.added) | copy-start | bytes 25165828
  87.4 1.0 copy-start.2

commit v2 on v1

--- a/solution.py
+++ b/solution.py
@@ -32,118 +32,210 @@
     return shot, slab, lax.rem(shot, 2), lax.rem(slab, 2)
 
 
-def gather_kernel(slabs, traces, cells, all_traces, all_cells, send, recv, own, pack_send, pack_recv, pack_own):
+def gather_kernel(
+    slabs, traces, cells, spots, all_traces, all_cells, all_spots, relay, send, recv, own, pair_send, pair_recv, pair_own
+):
     shot, slab, core, side = place()
     half = slabs // 2
     z = lax.div(slab, 2)
     stays = core == side
+    moves = core != side
+    other = (shot + 1 - 2 * core, slab)
     barrier = pltpu.get_barrier_semaphore()
+
+    def source_of(k):
+        return (shot - core + lax.rem(k, 2), k)
+
+    def is_source(k):
+        return jnp.logical_and(stays, k == slab)
 
     @pl.loop(0, slabs)
     def _(k):
-        @pl.when(jnp.logical_or(core != side, k != slab))
-        def _():
-            pl.semaphore_signal(barrier, inc=1, device_id=(shot - core + side, k), device_id_type=MESH)
-
-    pl.semaphore_wait(barrier, jnp.where(stays, slabs - 1, slabs))
-
-    def outgoing(k):
+        @pl.when(jnp.logical_not(is_source(k)))
+        def _():
+            pl.semaphore_signal(barrier, inc=1, device_id=source_of(k), device_id_type=MESH)
+
+    @pl.when(stays)
+    def _():
+        pl.semaphore_signal(barrier, inc=1, device_id=other, device_id_type=MESH)
+
+    pl.semaphore_wait(barrier, jnp.where(stays, 2 * slabs - 1, 1))
+
+    to_relay = pltpu.make_async_remote_copy(
+        src_ref=traces,
+        dst_ref=relay,
+        send_sem=pair_send.at[0],
+        recv_sem=pair_recv.at[0],
+        device_id=other,
+        device_id_type=MESH,
+    )
+    to_cells = pltpu.make_async_remote_copy(
+        src_ref=cells,
+        dst_ref=all_cells,
+        send_sem=pair_send.at[1],
+        recv_sem=pair_recv.at[1],
+        device_id=other,
+        device_id_type=MESH,
+    )
+    to_spots = pltpu.make_async_remote_copy(
+        src_ref=spots,
+        dst_ref=all_spots,
+        send_sem=pair_send.at[2],
+        recv_sem=pair_recv.at[2],
+        device_id=other,
+        device_id_type=MESH,
+    )
+    keep = (
+        pltpu.make_async_copy(traces, all_traces.at[slab], pair_own.at[0]),
+        pltpu.make_async_copy(cells, all_cells, pair_own.at[1]),
+        pltpu.make_async_copy(spots, all_spots, pair_own.at[2]),
+    )
+
+    def outgoing(here, n, k, to_side):
         to_core, to_z = lax.div(k, half), lax.rem(k, half)
         return pltpu.make_async_remote_copy(
-            src_ref=traces,
+            src_ref=here,
             dst_ref=all_traces.at[slab],
-            send_sem=send.at[k],
+            send_sem=send.at[n, k],
             recv_sem=recv.at[slab],
-            device_id=(shot - core + to_core, 2 * to_z + core),
+            device_id=(shot - core + to_core, 2 * to_z + to_side),
             device_id_type=MESH,
         )
 
     def is_me(k):
-        return jnp.logical_and(stays, k == core * half + z)
-
-    mine = pltpu.make_async_copy(traces, all_traces.at[slab], own.at[0])
-    pack = pltpu.make_async_remote_copy(
-        src_ref=cells,
-        dst_ref=all_cells,
-        send_sem=pack_send.at[0],
-        recv_sem=pack_recv.at[0],
-        device_id=(shot + 1 - 2 * core, slab),
-        device_id_type=MESH,
-    )
-    pack_mine = pltpu.make_async_copy(cells, all_cells, pack_own.at[0])
+        return k == core * half + z
+
+    @pl.when(moves)
+    def _():
+        to_relay.start()
 
     @pl.when(stays)
     def _():
-        pack.start()
-        pack_mine.start()
-        mine.start()
+        @pl.loop(0, slabs)
+        def _(k):
+            @pl.when(jnp.logical_not(is_me(k)))
+            def _():
+                outgoing(traces, 0, k, core).start()
+
+        to_cells.start()
+        to_spots.start()
+        for copy in keep:
+            copy.start()
+        to_relay.wait_recv()
+
+        @pl.loop(0, slabs)
+        def _(k):
+            outgoing(relay, 1, k, 1 - core).start()
 
     @pl.loop(0, slabs)
     def _(k):
-        @pl.when(jnp.logical_not(is_me(k)))
-        def _():
-            outgoing(k).start()
-
-    @pl.loop(0, slabs)
-    def _(k):
-        @pl.when(jnp.logical_or(core != side, k != slab))
+        @pl.when(jnp.logical_not(is_source(k)))
         def _():
             pltpu.make_async_remote_copy(
-                src_ref=traces,
+                src_ref=relay,
                 dst_ref=all_traces.at[k],
-                send_sem=send.at[k],
+                send_sem=send.at[0, k],
                 recv_sem=recv.at[k],
-                device_id=(shot - core + side, k),
+                device_id=source_of(k),
                 device_id_type=MESH,
             ).wait_recv()
 
-    @pl.loop(0, slabs)
-    def _(k):
-        @pl.when(jnp.logical_not(is_me(k)))
-        def _():
-            outgoing(k).wait_send()
+    @pl.when(moves)
+    def _():
+        to_relay.wait_send()
+        to_cells.wait_recv()
+        to_spots.wait_recv()
 
     @pl.when(stays)
     def _():
-        pack.wait_send()
-        pack_mine.wait()
-        mine.wait()
-
-    @pl.when(jnp.logical_not(stays))
-    def _():
-        pack.wait_recv()
-
-
-def inject_kernel(cells, keys, traces, out, listed):
-    @pl.loop(0, cells // 16)
+        to_cells.wait_send()
+        to_spots.wait_send()
+        for copy in keep:
+            copy.wait()
+
+        @pl.loop(0, slabs)
+        def _(k):
+            @pl.when(jnp.logical_not(is_me(k)))
+            def _():
+                outgoing(traces, 0, k, core).wait_send()
+
+            outgoing(relay, 1, k, 1 - core).wait_send()
+
+
+def inject_kernel(count, wide, steps, cells, traces, spots, out, amounts, mark, table, table_s, listed, sem):
+    shot, slab, core, side = place()
+    rows, lanes = cells.shape[1:]
+    lane = lax.broadcasted_iota(jnp.int32, (rows, lanes), 1)
+    order = lax.broadcasted_iota(jnp.int32, (rows, lanes), 0) * lanes + lane
+    depth = cells[0] - (slab - side + core) * count
+    live = jnp.logical_and(depth >= 0, depth < count)
+    key = jnp.where(live, order * (1 << 18) + (depth * wide + cells[1]) * 128 + cells[2], -1)
+
+    skipped = jnp.where(live, 0, 1)
+    for bit in range(7):
+        skipped = skipped + jnp.where(lane >= (1 << bit), pltpu.roll(skipped, 1 << bit, 1), 0)
+    table[rows : 2 * rows] = skipped
+    move = jnp.where(live, skipped, 0)
+    for bit in range(7):
+        from_key = pltpu.roll(key, 128 - (1 << bit), 1)
+        from_move = pltpu.roll(move, 128 - (1 << bit), 1)
+        comes = jnp.logical_and(
+            jnp.bitwise_and(from_move, 1 << bit) != 0, jnp.logical_and(from_key >= 0, lane < 128 - (1 << bit))
+        )
+        goes = jnp.bitwise_and(move, 1 << bit) != 0
+        key = jnp.where(comes, from_key, jnp.where(goes, -1, key))
+        move = jnp.where(comes, from_move, jnp.where(goes, 0, move))
+    table[0:rows] = key
+    copy = pltpu.make_async_copy(table, table_s, sem.at[0])
+    copy.start()
+
+    @pl.loop(0, count * wide // 32)
     def _(i):
-        out[pl.ds(pl.multiple_of(i * 128, 128), 128), :] = jnp.zeros((128, 128), F32)
-
-    rows, lanes = keys.shape
-
-    def compact(i, count):
-        for u in range(16):
-            key = keys[lax.shift_right_logical(i, 3), jnp.bitwise_and(i, 7) * 16 + u]
-            listed[count] = key
-            count = count + jnp.where(key >= 0, 1, 0).astype(jnp.int32)
-        return count
-
-    count = lax.fori_loop(0, rows * lanes // 16, compact, jnp.int32(0))
-    lane = lax.broadcasted_iota(jnp.int32, (8, 128), 1)
-
-    def add(k, carry):
-        key = listed[k]
-        r = lax.shift_right_logical(key, 18)
-        cell = jnp.bitwise_and(key, (1 << 18) - 1)
-        z = jnp.bitwise_and(cell, 127)
-        row = pl.multiple_of(lax.shift_right_logical(cell, 7) * 8, 8)
-        column = pl.multiple_of(jnp.bitwise_and(lax.shift_right_logical(r, 7), 1) * 128, 128)
-        values = traces[lax.shift_right_logical(r, 8), :, pl.ds(column, 128)]
-        turned = pltpu.roll(values, jnp.bitwise_and(z - jnp.bitwise_and(r, 127), 127), 1)
-        out[pl.ds(row, 8), :] = out[pl.ds(row, 8), :] + jnp.where(lane == z, turned, 0.0)
-        return carry
-
-    lax.fori_loop(0, count, add, jnp.int32(0))
+        out[pl.ds(pl.multiple_of(i * 256, 256), 256), :] = jnp.zeros((256, 128), F32)
+
+    plane = wide * 128
+    spot = jnp.broadcast_to(spots[:steps, 0:1], (steps, 128)).astype(jnp.int32) - (slab - side + core) * (count * plane)
+    wave = jnp.broadcast_to(spots[:steps, 1:2], (steps, 128))
+    tile_lane = lax.broadcasted_iota(jnp.int32, (8, 128), 1)
+    tile_cell = lax.broadcasted_iota(jnp.int32, (8, 128), 0) * 128 + tile_lane
+    for row in range(count):
+        hit = jnp.logical_and(spot >= row * plane, spot < (row + 1) * plane)
+        amounts[pl.ds(row * steps, steps), :] = jnp.where(hit, wave, 0.0)
+    place_in_plane = jnp.bitwise_and(spot, plane - 1)[:8]
+    for k in range(wide // 8):
+        mark[pl.ds(8 * k, 8), :] = jnp.where(tile_cell + 1024 * k == place_in_plane, 1.0, 0.0)
+
+    copy.wait()
+
+    def gather_row(i, base):
+        found = 128 - table_s[rows + i, 127]
+
+        @pl.loop(0, lax.div(found + 15, 16))
+        def _(k):
+            for u in range(16):
+                listed[base + 16 * k + u] = table_s[i, 16 * k + u]
+
+        return base + found
+
+    total = lax.fori_loop(0, rows, gather_row, jnp.int32(0))
+    for u in range(8):
+        listed[total + u] = -1
+
+    @pl.loop(0, lax.div(total + 7, 8))
+    def _(k):
+        places, values = [], []
+        for u in range(8):
+            key = listed[8 * k + u]
+            r = jnp.bitwise_and(lax.shift_right_logical(key, 18), rows * lanes - 1)
+            cell = jnp.bitwise_and(key, (1 << 18) - 1)
+            z = jnp.bitwise_and(cell, 127)
+            places.append(pl.multiple_of(lax.shift_right_logical(cell, 7) * 8, 8))
+            column = pl.multiple_of(jnp.bitwise_and(lax.shift_right_logical(r, 7), 1) * 128, 128)
+            held = traces[lax.shift_right_logical(r, 8), :, pl.ds(column, 128)]
+            turned = pltpu.roll(held, jnp.bitwise_and(z - jnp.bitwise_and(r, 127), 127), 1)
+            values.append(jnp.where(tile_lane == jnp.where(key >= 0, z, -1), turned, 0.0))
+        for where, value in zip(places, values):
+            out[pl.ds(where, 8), :] = out[pl.ds(where, 8), :] + value
 
 
 def wave_kernel(
@@ -359,9 +451,9 @@
             finish(4 * group + i, x[i], near + far * FAR + CENTRE * x[i])
 
     def depth(field, slot, base, planes, finish):
-        @pl.loop(0, wide // 8)
+        @pl.loop(0, wide // 16)
         def _(k):
-            part = pl.ds(pl.multiple_of(8 * k, 8), 8)
+            part = pl.ds(pl.multiple_of(16 * k, 16), 16)
             e = [field[slot, base + r, part, :] for r in range(planes + 2 * EDGE)]
             for r in range(planes):
                 value = (e[r + 3] + e[r + 5]) - 0.125 * (e[r + 2] + e[r + 6])
@@ -405,7 +497,7 @@
         keep = i if kept else lead
 
         def finish(row, x, value):
-            pf[i + 2, EDGE + row] = (2.0 * x - pf[i, EDGE + row]) + amounts[i, row] * mark[...]
+            pf[i + 2, EDGE + row] = (2.0 * x - pf[i, EDGE + row]) + amounts[pl.ds(row * steps + i, 1), :] * mark[...]
             laps[keep, row] = value
 
         @pl.loop(0, count // 4)
@@ -450,6 +542,7 @@
         spd[row] = UNIT * spd[row]
 
     inj_copy.wait()
+
     lateral_a(0)
 
     @pl.loop(0, lead)
@@ -639,7 +732,6 @@
     held = traces.shape[2]
     plane = wide * lanes
     shot, slab, core, side = place()
-    slab_here = slab - side + core
 
     over = ("shot", "slab")
     pairs, speed_pairs = [], []
@@ -655,57 +747,57 @@
     speed_far = lax.ppermute(speed_term, over, speed_pairs)
     after_far = lax.ppermute(adjoint_after[0], over, pairs)
 
-    flat = (receivers[0, 0] * plane + receivers[0, 1] * lanes + receivers[0, 2]).reshape(-1, 128)
-    spot = source[0, 0] * plane + source[0, 1] * lanes + source[0, 2]
-    cells = jnp.concatenate([flat, jnp.broadcast_to(spot, (8, 128))], axis=0)
-    wave = jnp.broadcast_to(wavelet[0][:, None], (steps, 128))
-    packed = jnp.concatenate([traces[0], wave], axis=1)
     anywhere = pl.BlockSpec(memory_space=pl.ANY)
     in_vmem = pl.BlockSpec(memory_space=pltpu.VMEM)
-    in_smem = pl.BlockSpec(memory_space=pltpu.SMEM)
-
-    all_traces, all_cells = pl.pallas_call(
+    cells = receivers.reshape(3, -1, 128)
+    spot = source[0, 0] * plane + source[0, 1] * lanes + source[0, 2]
+    which = lax.broadcasted_iota(jnp.int32, (2 * steps, 128), 1)
+    wave = jnp.concatenate([wavelet[0], wavelet[0]])[:, None]
+    spots = jnp.where(which == 0, spot.astype(F32), wave)
+
+    all_traces, all_cells, all_spots = pl.pallas_call(
         functools.partial(gather_kernel, slabs),
         name="gather_traces",
         out_shape=(
-            jax.ShapeDtypeStruct((slabs, steps, held + 128), F32),
+            jax.ShapeDtypeStruct((slabs, steps, held), F32),
             jax.ShapeDtypeStruct(cells.shape, jnp.int32),
+            jax.ShapeDtypeStruct(spots.shape, F32),
         ),
-        in_specs=[anywhere, anywhere],
-        out_specs=(anywhere, anywhere),
+        in_specs=[anywhere, anywhere, anywhere],
+        out_specs=(in_vmem, in_vmem, in_vmem),
         scratch_shapes=[
-            pltpu.SemaphoreType.DMA((slabs,)),
+            pltpu.VMEM((steps, held), F32),
+            pltpu.SemaphoreType.DMA((2, slabs)),
             pltpu.SemaphoreType.DMA((slabs,)),
             pltpu.SemaphoreType.DMA((1,)),
-            pltpu.SemaphoreType.DMA((1,)),
-            pltpu.SemaphoreType.DMA((1,)),
+            pltpu.SemaphoreType.DMA((3,)),
+            pltpu.SemaphoreType.DMA((3,)),
+            pltpu.SemaphoreType.DMA((3,)),
+        ],
+        compiler_params=pltpu.CompilerParams(collective_id=0, has_side_effects=True, vmem_limit_bytes=8 << 20),
+        cost_estimate=pl.CostEstimate(flops=0, bytes_accessed=20 << 20, transcendentals=0),
+    )(traces[0], cells, spots)
+
+    added, amounts, mark = pl.pallas_call(
+        functools.partial(inject_kernel, count, wide, steps),
+        name="inject",
+        out_shape=(
+            jax.ShapeDtypeStruct((count * wide * steps, lanes), F32),
+            jax.ShapeDtypeStruct((count * steps, lanes), F32),
+            jax.ShapeDtypeStruct((wide, lanes), F32),
+        ),
+        in_specs=[in_vmem, in_vmem, in_vmem],
+        out_specs=(in_vmem, in_vmem, in_vmem),
+        scratch_shapes=[
+            pltpu.VMEM((2 * cells.shape[1], 128), jnp.int32),
+            pltpu.SMEM((2 * cells.shape[1], 128), jnp.int32),
+            pltpu.SMEM((cells.size // 3 + 32,), jnp.int32),
             pltpu.SemaphoreType.DMA((1,)),
         ],
-        compiler_params=pltpu.CompilerParams(collective_id=0, has_side_effects=True),
-        cost_estimate=pl.CostEstimate(flops=0, bytes_accessed=20 << 20, transcendentals=0),
-    )(packed, cells)
-
-    base = slab_here * (count * plane)
-    here = all_cells[:-8] - base
-    order = lax.broadcasted_iota(jnp.int32, here.shape, 0) * 128 + lax.broadcasted_iota(jnp.int32, here.shape, 1)
-    keys = jnp.where((here >= 0) & (here < count * plane), order * (count * plane) + here, -1)
-    added = pl.pallas_call(
-        functools.partial(inject_kernel, count * wide),
-        name="inject",
-        out_shape=jax.ShapeDtypeStruct((count * wide * steps, lanes), F32),
-        in_specs=[in_smem, in_vmem],
-        out_specs=in_vmem,
-        scratch_shapes=[pltpu.SMEM((here.size,), jnp.int32)],
-        compiler_params=pltpu.CompilerParams(vmem_limit_bytes=32 << 20),
+        compiler_params=pltpu.CompilerParams(vmem_limit_bytes=20 << 20),
         cost_estimate=pl.CostEstimate(flops=0, bytes_accessed=30 << 20, transcendentals=0),
-    )(keys, all_traces)
-
-    spot_here = all_cells[-1, 0] - base
-    spot_row = jnp.where(spot_here < 0, -1, spot_here // plane)
-    spot_cell = jnp.bitwise_and(spot_here, plane - 1)
-    amounts = jnp.where(lax.broadcasted_iota(jnp.int32, (steps, count), 1) == spot_row, all_traces[0, :, held : held + 1], 0.0)
-    mark_at = lax.broadcasted_iota(jnp.int32, (wide, lanes), 0) * lanes + lax.broadcasted_iota(jnp.int32, (wide, lanes), 1)
-    mark = jnp.where(mark_at == spot_cell, 1.0, 0.0).astype(F32)
+    )(all_cells, all_traces, all_spots)
+
     weights = band(wide)
 
     long = count + 2 * EDGE
@@ -717,8 +809,8 @@
             jax.ShapeDtypeStruct((1, count, wide, lanes), F32),
             jax.ShapeDtypeStruct((count, wide // shots, lanes), F32),
         ),
-        in_specs=[anywhere] * 9 + [in_smem, in_vmem, in_vmem, in_vmem],
-        out_specs=(anywhere, anywhere, in_vmem),
+        in_specs=[anywhere] * 9 + [in_vmem] * 4,
+        out_specs=(in_vmem, in_vmem, in_vmem),
         scratch_shapes=[
             pltpu.VMEM((steps + 2, long, wide, lanes), F32),
             pltpu.VMEM((steps + 2, long, wide, lanes), F32),
@@ -739,7 +831,7 @@
             pltpu.SemaphoreType.DMA((3,)),
         ],
         compiler_params=pltpu.CompilerParams(
-            collective_id=1, has_side_effects=True, vmem_limit_bytes=62 << 20
+            collective_id=1, has_side_effects=True, vmem_limit_bytes=51 << 20
         ),
     )(
         adjoint_now[0],

time: 189 us -> 134 us (0.71)
  Pallas kernels: 161 us -> 116 us
  other arithmetic: 4.27 us -> 0.89 us
  local copies, waits for them, and re-layouts: 15.2 us -> 12.2 us
  starting transfers between devices: 4.07 us -> 2.18 us
    pallas_call x1, Pallas kernels: 48.3 us -> 9.68 us  [body(): pl.pallas_call(functools.partial(inject_kernel, count, wide, steps), name...]
    pallas_call x1, Pallas kernels: 93.1 us -> 85.9 us  [body(): pl.pallas_call(functools.partial(wave_kernel, shots, slabs, steps, UNIT /...]
    select_n x3 -> x1, other arithmetic: 2.18 us -> 0.07 us  [body(): spots = jnp.where(which == 0, spot.astype(F32), wave)]
    unnamed x9 -> x19, local copies, waits for them, and re-layouts: 11.2 us -> 10.8 us
  transfers between devices with their start and end apart: 3 -> 3, of which waited for: 0 -> 0; matrix products, arithmetic and copies ran while one was open for 4% -> 2% of each run, Pallas kernels for 36% -> 22%
where the time goes in v2:
time: 134 us; the launch traced here: 133 us
  Pallas kernels  116 us (87%)
  local copies, waits for them, and re-layouts  12.2 us (9%)
  between operations  2.68 us (2%)
  starting transfers between devices  2.18 us (2%)
    pallas_call x1, Pallas kernels, body(): pl.pallas_call(functools.partial(wave_kernel, shots, slabs, steps, UNIT /...  85.9 us
    pallas_call x1, Pallas kernels, body(): pl.pallas_call(functools.partial(gather_kernel, slabs), name='gather_trac...  20 us
    unnamed x19, local copies, waits for them, and re-layouts  10.8 us
    pallas_call x1, Pallas kernels, body(): pl.pallas_call(functools.partial(inject_kernel, count, wide, steps), name...  9.68 us
  transfers between devices with their start and end apart: 3, of which 0 were waited for; matrix products, arithmetic and copies ran while one was open for 2% of the time, Pallas kernels for 22%

profile of v2, /device:TPU:32, one launch (start us, length us, event | category | flops | bytes accessed | tf_op | source)
XLA Modules:
  0.0 133.4 jit_solution(2836946008066610734)
XLA Ops:
  0.6 0.7 collective-permute-start.1
  1.4 0.7 collective-permute-start
  2.1 0.7 collective-permute-start.2
  2.8 1.4 %fusion = (s32[1,1]{1,0:T(1,128)}, s32[1,1]{1,0:T(1,128)}, s32[1,1]{1,0:T(1,128)}) fusion(s32[1,3]{1,0:T(1,128)} %param.17), kind=kLoop, calls=%fused_computation.3 | loop fusion | bytes 24 | tf_op jit(solution)/shard_map/slice | solution.py:753
  6.2 0.8 pad_maximum_fusion
  7.0 0.1 broadcast_select_fusion.spots
  7.0 0.8 copy-done.3
  7.8 0.7 copy-done.4
  8.5 20.0 %gather_traces.1 = (f32[16,8,256]{2,1,0:T(8,128)S(1)}, s32[3,32,128]{2,1,0:T(8,128)S(1)}, f32[16,128]{1,0:T(8,128)S(1)}) custom-call(f32[8,256]{1,0:T(8,128)S(1)} %bitcast.9, s32[3,32,128]{2,1,0:T(8,128)S(1)} %bitcast.8, f32[16,128]{1,0:T(8,128)S(1)} %broadcast_select_fusion.spots), custom_call_target="tpu_custom_call" | custom-call | bytes 20971520 | tf_op jit(solution)/shard_map/gather_traces/pallas_call | solution.py:758
  28.5 9.7 %inject.1 = (f32[16384,128]{1,0:T(8,128)S(1)}, f32[128,128]{1,0:T(8,128)S(1)}, f32[128,128]{1,0:T(8,128)S(1)}) custom-call(s32[3,32,128]{2,1,0:T(8,128)S(1)} %get-tuple-element.9.cells, f32[16,8,256]{2,1,0:T(8,128)S(1)} %get-tuple-element.10.traces, f32[16,128]{1,0:T(8,128)S(1)} %get-tuple-element.11.spots), custom_call_target="tpu_custom_call" | custom-call | bytes 31457280 | tf_op jit(solution)/shard_map/inject/pallas_call | solution.py:781
  38.2 3.2 %copy-done = f32[16384,128]{1,0:T(8,128)} copy-done((f32[16384,128]{1,0:T(8,128)}, f32[16384,128]{1,0:T(8,128)S(1)}, u32[]{:S(2)}) %copy-start) | copy-done | bytes 8388632
  41.4 0.0 collective-permute-done.1.adj_after_far
  41.4 0.0 collective-permute-done.adj_now_far
  41.4 0.0 copy-start.6
  41.4 0.0 collective-permute-done.2.speed_far
  41.5 0.9 copy-done.5
  42.4 0.3 copy-done.6
  42.7 0.4 copy-done.7
  43.2 0.9 copy-done.1
  44.1 0.9 copy-done.2
  45.0 85.9 %waves.1 = (f32[1,16,128,128]{3,2,1,0:T(8,128)S(1)}, f32[1,16,128,128]{3,2,1,0:T(8,128)S(1)}, f32[16,8,128]{2,1,0:T(8,128)S(1)}) custom-call(f32[16,128,128]{2,1,0:T(8,128)} %bitcast.11, f32[16,128,128]{2,1,0:T(8,128)} %copy-done.6, f32[16,128,128]{2,1,0:T(8,128)} %bitcast.13, f32[16,128,128]{2,1,0:T(8,128)} %copy-done.5, f32[16,128,128]{2,1,0:T(8,128)} %bitcast.14, ...), custom_call_target="tpu_custom_call" | custom-call | tf_op jit(solution)/shard_map/waves/pallas_call | solution.py:804
  130.9 1.0 copy.17
  131.8 1.0 copy.18
  132.8 0.6 copy.19
  (8 shorter events, 0.0 us)
Async XLA Ops:
  0.6 40.8 %collective-permute-start.1 = (f32[16,128,128]{2,1,0:T(8,128)}, f32[16,128,128]{2,1,0:T(8,128)S(1)}, u32[]{:S(2)}, u32[]{:S(2)}) collective-permute-start(f32[16,128,128]{2,1,0:T(8,128)} %bitcast.12), channel_id=1, source_target_pairs={{1,16},{3,18},{5,20},{7,22},{9,24},{11,26},{13,28},{15,30},{16,1},... | collective-permute-start | bytes 3145736 | tf_op jit(solution)/shard_map/ppermute | solution.py:748
  1.4 40.1 %collective-permute-start = (f32[16,128,128]{2,1,0:T(8,128)}, f32[16,128,128]{2,1,0:T(8,128)S(1)}, u32[]{:S(2)}, u32[]{:S(2)}) collective-permute-start(f32[16,128,128]{2,1,0:T(8,128)} %bitcast.10), channel_id=1, source_target_pairs={{1,16},{3,18},{5,20},{7,22},{9,24},{11,26},{13,28},{15,30},{16,1},... | collective-permute-start | bytes 3145736 | tf_op jit(solution)/shard_map/ppermute | solution.py:746
  2.1 39.3 %collective-permute-start.2 = (f32[16,128,128]{2,1,0:T(8,128)}, f32[16,128,128]{2,1,0:T(8,128)S(1)}, u32[]{:S(2)}, u32[]{:S(2)}) collective-permute-start(f32[16,128,128]{2,1,0:T(8,128)} %speed.1), channel_id=1, source_target_pairs={{1,48},{3,50},{5,52},{7,54},{9,56},{11,58},{13,60},{15,62},{16,33}... | collective-permute-start | bytes 3145736 | tf_op jit(solution)/shard_map/ppermute | solution.py:747
  7.0 0.8 copy-start.3
  7.8 0.7 copy-start.4
  38.2 3.2 %copy-start = (f32[16384,128]{1,0:T(8,128)}, f32[16384,128]{1,0:T(8,128)S(1)}, u32[]{:S(2)}) copy-start(f32[16384,128]{1,0:T(8,128)S(1)} %get-tuple-element.12.added) | copy-start | bytes 25165828
  41.4 1.0 copy-start.5
  41.4 1.3 copy-start.6
  41.5 1.7 %copy-start.7 = (f32[16,128,128]{2,1,0:T(8,128)}, f32[16,128,128]{2,1,0:T(8,128)S(1)}, u32[]{:S(2)}) copy-start(f32[16,128,128]{2,1,0:T(8,128)S(1)} %collective-permute-done.2.speed_far) | copy-start | bytes 3145732
  43.2 0.9 copy-start.1
  44.1 0.9 copy-start.2

commit v3 on v2

--- a/solution.py
+++ b/solution.py
@@ -1,6 +1,5 @@
 import functools
 
-import numpy as np
 import jax
 import jax.numpy as jnp
 from jax import lax
@@ -18,14 +17,6 @@
 EDGE = 4
 
 
-def band(width):
-    gap = np.abs(np.arange(width)[:, None] - np.arange(width)[None, :])
-    near = np.where(gap == 1, 1.0, 0.0) + np.where(gap == 2, -1.0 / 8.0, 0.0)
-    far = np.where(gap == 3, 1.0, 0.0) + np.where(gap == 4, -9.0 / 128.0, 0.0)
-    row = np.concatenate([near, far], axis=1)
-    return np.concatenate([row, row], axis=0)
-
-
 def place():
     shot = lax.axis_index("shot")
     slab = lax.axis_index("slab")
@@ -33,7 +24,27 @@
 
 
 def gather_kernel(
-    slabs, traces, cells, spots, all_traces, all_cells, all_spots, relay, send, recv, own, pair_send, pair_recv, pair_own
+    slabs,
+    wide,
+    lanes,
+    traces,
+    cells,
+    source,
+    wavelet,
+    field,
+    all_traces,
+    all_cells,
+    all_spots,
+    field_far,
+    relay,
+    spots,
+    send,
+    recv,
+    pair_send,
+    pair_recv,
+    pair_own,
+    swap_send,
+    swap_recv,
 ):
     shot, slab, core, side = place()
     half = slabs // 2
@@ -59,7 +70,21 @@
     def _():
         pl.semaphore_signal(barrier, inc=1, device_id=other, device_id_type=MESH)
 
-    pl.semaphore_wait(barrier, jnp.where(stays, 2 * slabs - 1, 1))
+    partner = (shot - core + side, slab - side + core)
+
+    @pl.when(moves)
+    def _():
+        pl.semaphore_signal(barrier, inc=1, device_id=partner, device_id_type=MESH)
+
+    steps = spots.shape[0]
+    step_of = lax.broadcasted_iota(jnp.int32, spots.shape, 0)
+    wave = jnp.zeros(spots.shape, F32)
+    for t in range(steps):
+        wave = jnp.where(step_of == t, wavelet[0, t], wave)
+    cell = (source[0, 0] * (wide * lanes) + source[0, 1] * lanes + source[0, 2]).astype(F32)
+    spots[...] = jnp.where(lax.broadcasted_iota(jnp.int32, spots.shape, 1) == 0, cell, wave)
+
+    pl.semaphore_wait(barrier, jnp.where(stays, 2 * slabs - 1, 2))
 
     to_relay = pltpu.make_async_remote_copy(
         src_ref=traces,
@@ -105,9 +130,19 @@
     def is_me(k):
         return k == core * half + z
 
+    swap = pltpu.make_async_remote_copy(
+        src_ref=field,
+        dst_ref=field_far,
+        send_sem=swap_send.at[0],
+        recv_sem=swap_recv.at[0],
+        device_id=partner,
+        device_id_type=MESH,
+    )
+
     @pl.when(moves)
     def _():
         to_relay.start()
+        swap.start()
 
     @pl.when(stays)
     def _():
@@ -142,6 +177,7 @@
 
     @pl.when(moves)
     def _():
+        swap.wait()
         to_relay.wait_send()
         to_cells.wait_recv()
         to_spots.wait_recv()
@@ -162,7 +198,7 @@
             outgoing(relay, 1, k, 1 - core).wait_send()
 
 
-def inject_kernel(count, wide, steps, cells, traces, spots, out, amounts, mark, table, table_s, listed, sem):
+def inject_kernel(count, wide, steps, cells, traces, spots, out, table, table_s, listed, sem):
     shot, slab, core, side = place()
     rows, lanes = cells.shape[1:]
     lane = lax.broadcasted_iota(jnp.int32, (rows, lanes), 1)
@@ -200,10 +236,10 @@
     tile_cell = lax.broadcasted_iota(jnp.int32, (8, 128), 0) * 128 + tile_lane
     for row in range(count):
         hit = jnp.logical_and(spot >= row * plane, spot < (row + 1) * plane)
-        amounts[pl.ds(row * steps, steps), :] = jnp.where(hit, wave, 0.0)
+        out[pl.ds(count * wide * steps + row * steps, steps), :] = jnp.where(hit, wave, 0.0)
     place_in_plane = jnp.bitwise_and(spot, plane - 1)[:8]
     for k in range(wide // 8):
-        mark[pl.ds(8 * k, 8), :] = jnp.where(tile_cell + 1024 * k == place_in_plane, 1.0, 0.0)
+        out[pl.ds(count * (wide + 1) * steps + 8 * k, 8), :] = jnp.where(tile_cell + 1024 * k == place_in_plane, 1.0, 0.0)
 
     copy.wait()
 
@@ -252,10 +288,6 @@
     speed,
     speed_far,
     added,
-    amounts,
-    mark,
-    weights_z,
-    weights_y,
     opening,
     second,
     gradient,
@@ -266,6 +298,8 @@
     spd,
     total,
     parts,
+    weights_z,
+    weights_y,
     loads,
     swap_send,
     swap_recv,
@@ -385,6 +419,16 @@
                 qa[k + 1, row] = jnp.zeros((wide, lanes), F32)
                 pf[k + 1, row] = jnp.zeros((wide, lanes), F32)
 
+    for across, ref in enumerate((weights_z, weights_y)):
+        inside = lax.broadcasted_iota(jnp.int32, (2 * wide, 2 * wide), 0)
+        given = lax.broadcasted_iota(jnp.int32, (2 * wide, 2 * wide), 1)
+        if across:
+            inside, given = given, inside
+        gap = jnp.abs(lax.rem(inside, wide) - lax.rem(given, wide))
+        near = jnp.where(gap == 1, 1.0, jnp.where(gap == 2, -1.0 / 8.0, 0.0))
+        far = jnp.where(gap == 3, 1.0, jnp.where(gap == 4, -9.0 / 128.0, 0.0))
+        ref[...] = jnp.where(given < wide, near, far).astype(BF16)
+
     pl.semaphore_wait(
         barrier,
         1 + jnp.where(has_outer, 1, 0) + jnp.where(moves, 1, 0) + jnp.where(stays, shots - 1, shots),
@@ -428,6 +472,8 @@
         def _():
             outer_copy(chain, slot).wait_recv()
 
+    amounts_at = count * wide * steps
+    mark_at = amounts_at + count * steps
     inner_base = (1 - core) * (mid + EDGE)
     outer_base = core * (mid + EDGE)
 
@@ -497,7 +543,7 @@
         keep = i if kept else lead
 
         def finish(row, x, value):
-            pf[i + 2, EDGE + row] = (2.0 * x - pf[i, EDGE + row]) + amounts[pl.ds(row * steps + i, 1), :] * mark[...]
+            pf[i + 2, EDGE + row] = (2.0 * x - pf[i, EDGE + row]) + inj[pl.ds(amounts_at + row * steps + i, 1), :] * inj[pl.ds(mark_at, wide), :]
             laps[keep, row] = value
 
         @pl.loop(0, count // 4)
@@ -743,62 +789,57 @@
                 high = (s // 2) % 2
                 other = s - 2 * high + 2 * (1 - high) - c + d
                 speed_pairs.append((s * slabs + k, other * slabs + k - d + c))
-    now_far = lax.ppermute(adjoint_now[0], over, pairs)
-    speed_far = lax.ppermute(speed_term, over, speed_pairs)
-    after_far = lax.ppermute(adjoint_after[0], over, pairs)
-
     anywhere = pl.BlockSpec(memory_space=pl.ANY)
     in_vmem = pl.BlockSpec(memory_space=pltpu.VMEM)
+    in_smem = pl.BlockSpec(memory_space=pltpu.SMEM)
     cells = receivers.reshape(3, -1, 128)
-    spot = source[0, 0] * plane + source[0, 1] * lanes + source[0, 2]
-    which = lax.broadcasted_iota(jnp.int32, (2 * steps, 128), 1)
-    wave = jnp.concatenate([wavelet[0], wavelet[0]])[:, None]
-    spots = jnp.where(which == 0, spot.astype(F32), wave)
-
-    all_traces, all_cells, all_spots = pl.pallas_call(
-        functools.partial(gather_kernel, slabs),
+
+    all_traces, all_cells, all_spots, now_far = pl.pallas_call(
+        functools.partial(gather_kernel, slabs, wide, lanes),
         name="gather_traces",
         out_shape=(
             jax.ShapeDtypeStruct((slabs, steps, held), F32),
             jax.ShapeDtypeStruct(cells.shape, jnp.int32),
-            jax.ShapeDtypeStruct(spots.shape, F32),
+            jax.ShapeDtypeStruct((steps, 128), F32),
+            jax.ShapeDtypeStruct(speed_term.shape, F32),
         ),
-        in_specs=[anywhere, anywhere, anywhere],
-        out_specs=(in_vmem, in_vmem, in_vmem),
+        in_specs=[anywhere, anywhere, in_smem, in_smem, anywhere],
+        out_specs=(in_vmem, in_vmem, in_vmem, anywhere),
         scratch_shapes=[
             pltpu.VMEM((steps, held), F32),
+            pltpu.VMEM((steps, 128), F32),
             pltpu.SemaphoreType.DMA((2, slabs)),
             pltpu.SemaphoreType.DMA((slabs,)),
-            pltpu.SemaphoreType.DMA((1,)),
             pltpu.SemaphoreType.DMA((3,)),
             pltpu.SemaphoreType.DMA((3,)),
             pltpu.SemaphoreType.DMA((3,)),
+            pltpu.SemaphoreType.DMA((1,)),
+            pltpu.SemaphoreType.DMA((1,)),
         ],
-        compiler_params=pltpu.CompilerParams(collective_id=0, has_side_effects=True, vmem_limit_bytes=8 << 20),
+        compiler_params=pltpu.CompilerParams(collective_id=0, has_side_effects=True, vmem_limit_bytes=67_000_000),
         cost_estimate=pl.CostEstimate(flops=0, bytes_accessed=20 << 20, transcendentals=0),
-    )(traces[0], cells, spots)
-
-    added, amounts, mark = pl.pallas_call(
+    )(traces[0], cells, source, wavelet, adjoint_now[0])
+
+    after, here_speed, all_traces = lax.optimization_barrier((adjoint_after[0], speed_term, all_traces))
+    after_far = lax.ppermute(after, over, pairs)
+    speed_far = lax.ppermute(here_speed, over, speed_pairs)
+
+    held_rows = count * (wide + 1) * steps + wide
+    added = pl.pallas_call(
         functools.partial(inject_kernel, count, wide, steps),
         name="inject",
-        out_shape=(
-            jax.ShapeDtypeStruct((count * wide * steps, lanes), F32),
-            jax.ShapeDtypeStruct((count * steps, lanes), F32),
-            jax.ShapeDtypeStruct((wide, lanes), F32),
-        ),
+        out_shape=jax.ShapeDtypeStruct((held_rows, lanes), F32),
         in_specs=[in_vmem, in_vmem, in_vmem],
-        out_specs=(in_vmem, in_vmem, in_vmem),
+        out_specs=in_vmem,
         scratch_shapes=[
             pltpu.VMEM((2 * cells.shape[1], 128), jnp.int32),
             pltpu.SMEM((2 * cells.shape[1], 128), jnp.int32),
             pltpu.SMEM((cells.size // 3 + 32,), jnp.int32),
             pltpu.SemaphoreType.DMA((1,)),
         ],
-        compiler_params=pltpu.CompilerParams(vmem_limit_bytes=20 << 20),
+        compiler_params=pltpu.CompilerParams(vmem_limit_bytes=67_000_000),
         cost_estimate=pl.CostEstimate(flops=0, bytes_accessed=30 << 20, transcendentals=0),
     )(all_cells, all_traces, all_spots)
-
-    weights = band(wide)
 
     long = count + 2 * EDGE
     opening, second, gradient = pl.pallas_call(
@@ -809,16 +850,18 @@
             jax.ShapeDtypeStruct((1, count, wide, lanes), F32),
             jax.ShapeDtypeStruct((count, wide // shots, lanes), F32),
         ),
-        in_specs=[anywhere] * 9 + [in_vmem] * 4,
+        in_specs=[anywhere] * 9,
         out_specs=(in_vmem, in_vmem, in_vmem),
         scratch_shapes=[
             pltpu.VMEM((steps + 2, long, wide, lanes), F32),
             pltpu.VMEM((steps + 2, long, wide, lanes), F32),
             pltpu.VMEM((steps // 2 + 1, count, wide, lanes), F32),
-            pltpu.VMEM((count * wide * steps, lanes), F32),
+            pltpu.VMEM((held_rows, lanes), F32),
             pltpu.VMEM((count, wide, lanes), F32),
             pltpu.VMEM((count, wide, lanes), F32),
             pltpu.VMEM((shots, count, wide // shots, lanes), F32),
+            pltpu.VMEM((2 * wide, 2 * wide), BF16),
+            pltpu.VMEM((2 * wide, 2 * wide), BF16),
             pltpu.SemaphoreType.DMA((8,)),
             pltpu.SemaphoreType.DMA((2,)),
             pltpu.SemaphoreType.DMA((2,)),
@@ -843,10 +886,6 @@
         speed_term,
         speed_far,
         added,
-        amounts,
-        mark,
-        jnp.asarray(weights, BF16),
-        jnp.asarray(weights.T, BF16),
     )
     return opening, second, gradient
 

time: 134 us -> 132 us (0.985)
  the two profiles are of different devices: /device:TPU:32 before, /device:TPU:103 now
where the time goes in v3:
time: 132 us
  Pallas kernels  125 us (95%)
  starting transfers between devices  3.26 us (2%)
  local copies, waits for them, and re-layouts  2.57 us (2%)
    pallas_call x1, Pallas kernels, body(): pl.pallas_call(functools.partial(wave_kernel, shots, slabs, steps, UNIT /...  100 us
    pallas_call x1, Pallas kernels, body(): pl.pallas_call(functools.partial(gather_kernel, slabs, wide, lanes), name...  13.6 us
    pallas_call x1, Pallas kernels, body(): pl.pallas_call(functools.partial(inject_kernel, count, wide, steps), name...  11.3 us
  transfers between devices with their start and end apart: 2, of which 0 were waited for; matrix products, arithmetic and copies ran while one was open for 0% of the time, Pallas kernels for 9%

profile of v3, /device:TPU:103, one launch (start us, length us, event | category | flops | bytes accessed | tf_op | source)
XLA Modules:
  0.0 131.7 jit_solution(16134365429910633681)
XLA Ops:
  0.6 13.6 %gather_traces.1 = (f32[16,8,256]{2,1,0:T(8,128)}, s32[3,32,128]{2,1,0:T(8,128)}, f32[8,128]{1,0:T(8,128)}, f32[16,128,128]{2,1,0:T(8,128)}) custom-call(f32[8,256]{1,0:T(8,128)} %bitcast.13, s32[3,32,128]{2,1,0:T(8,128)} %bitcast.12, s32[1,3]{1,0:T(1,128)} %source.1, f32[1,8]{1,0:T(1,128)} %wavelet.1, f32[16,128,128]{2,1,0:T(8,128)} %bitcast.6), custom_call_target="tpu_custom_call" | custom-call | bytes 20971520 | tf_op jit(solution)/shard_map/gather_traces/pallas_call | solution.py:797
  14.2 1.6 %collective-permute-start = (f32[16,128,128]{2,1,0:T(8,128)}, f32[16,128,128]{2,1,0:T(8,128)}, u32[]{:S(2)}, u32[]{:S(2)}) collective-permute-start(f32[16,128,128]{2,1,0:T(8,128)} %bitcast.8), channel_id=1, source_target_pairs={{1,16},{3,18},{5,20},{7,22},{9,24},{11,26},{13,28},{15,30},{16,1},... | collective-permute-start | bytes 3145736 | tf_op jit(solution)/shard_map/ppermute | solution.py:824
  15.8 1.6 %collective-permute-start.1 = (f32[16,128,128]{2,1,0:T(8,128)}, f32[16,128,128]{2,1,0:T(8,128)}, u32[]{:S(2)}, u32[]{:S(2)}) collective-permute-start(f32[16,128,128]{2,1,0:T(8,128)} %speed.1), channel_id=1, source_target_pairs={{1,48},{3,50},{5,52},{7,54},{9,56},{11,58},{13,60},{15,62},{16,33}... | collective-permute-start | bytes 3145736 | tf_op jit(solution)/shard_map/ppermute | solution.py:825
  17.5 11.3 %inject.1.added = f32[16640,128]{1,0:T(8,128)} custom-call(s32[3,32,128]{2,1,0:T(8,128)} %get-tuple-element.14.cells, f32[16,8,256]{2,1,0:T(8,128)} %get-tuple-element.15.traces, f32[8,128]{1,0:T(8,128)} %get-tuple-element.16.spots), custom_call_target="tpu_custom_call" | custom-call | bytes 31457280 | tf_op jit(solution)/shard_map/inject/pallas_call | solution.py:828
  28.8 0.0 collective-permute-done.adj_after_far
  28.8 0.0 collective-permute-done.1.speed_far
  28.8 100.3 %waves.1 = (f32[1,16,128,128]{3,2,1,0:T(8,128)S(1)}, f32[1,16,128,128]{3,2,1,0:T(8,128)S(1)}, f32[16,8,128]{2,1,0:T(8,128)S(1)}) custom-call(f32[16,128,128]{2,1,0:T(8,128)} %bitcast.7, f32[16,128,128]{2,1,0:T(8,128)} %get-tuple-element.10.adj_now_far, f32[16,128,128]{2,1,0:T(8,128)} %bitcast.9, f32[16,128,128]{2,1,0:T(8,128)} %collective-permute-done.adj_after_far, ...), custom_call_target="tpu_custom_call" | custom-call | tf_op jit(solution)/shard_map/waves/pallas_call | solution.py:845
  129.2 1.0 copy.15
  130.1 1.0 copy.16
  131.1 0.6 copy.17
Async XLA Ops:
  14.2 14.6 %collective-permute-start = (f32[16,128,128]{2,1,0:T(8,128)}, f32[16,128,128]{2,1,0:T(8,128)}, u32[]{:S(2)}, u32[]{:S(2)}) collective-permute-start(f32[16,128,128]{2,1,0:T(8,128)} %bitcast.8), channel_id=1, source_target_pairs={{1,16},{3,18},{5,20},{7,22},{9,24},{11,26},{13,28},{15,30},{16,1},... | collective-permute-start | bytes 3145736 | tf_op jit(solution)/shard_map/ppermute | solution.py:824
  15.8 13.0 %collective-permute-start.1 = (f32[16,128,128]{2,1,0:T(8,128)}, f32[16,128,128]{2,1,0:T(8,128)}, u32[]{:S(2)}, u32[]{:S(2)}) collective-permute-start(f32[16,128,128]{2,1,0:T(8,128)} %speed.1), channel_id=1, source_target_pairs={{1,48},{3,50},{5,52},{7,54},{9,56},{11,58},{13,60},{15,62},{16,33}... | collective-permute-start | bytes 3145736 | tf_op jit(solution)/shard_map/ppermute | solution.py:825
